TPU v7x, 32 devices: a whole 2x2x4 slice. The times are simulated.
32 devices in a mesh: sub: 4 (over y, x), tile: 8 (over z, core).
Axes of the slice: x: 2, y: 2, z: 4, core: 2. Of those that a mesh axis runs over, the one named last changes fastest.
Arguments:
- echoes: bfloat16 [2, 2048, 16384], P(None, 'sub', 'tile'), may hold values from -6 to 6
- steering: bfloat16 [2, 2048, 64], P(None, ('sub', 'tile')), may hold values from -0.5 to 0.5
- interp: bfloat16 [81920], replicated, may hold values from -6 to 6
- angles: float32 [8, 4, 2, 2, 16384], P('tile', 'sub'), may hold values from -3.140625 to 3.140625
- range_map: bfloat16 [8, 16384, 1024], P('tile', 'sub'), may hold values from -0.0234375 to 0.0234375
- beam_map: bfloat16 [8, 8, 256, 256], P('tile'), may hold values from -0.375 to 0.375
- footprint: int32 [8, 4], P('tile'), may hold values from 0 to 7, all different within a row
Outputs:
- image_tile: float32 [2, 2048, 1024], P(None, 'tile', 'sub')
Inputs may be any that keep to these rules, and one draw needn't show every extreme that they name: `footprint`: each row names 4 different tiles, and every tile is named by some row.
All inputs are finite; a program needn't handle non-finite values.
Results may differ from a plain program's by a relative error of at most 0.018.
Values may be sent and summed in bfloat16 or wider, within the bound.
No kernel may reach another device: no remote copies, remote signals or barrier semaphores. Data moves between devices by JAX's collectives and lax.ppermute only.
A program may use at most 128 MiB of HBM per device.

v0:
```python
import functools

import jax
import jax.numpy as jnp
from jax import lax
from jax.experimental import pallas as pl
from jax.experimental.pallas import tpu as pltpu
from jax.sharding import PartitionSpec as P


SHARES = (0, 7 / 16, 10 / 16, 13 / 16, 1)
GRANT = 24 << 20


def swap(block, axis, mask):
    count = lax.axis_size(axis)
    return lax.ppermute(block, axis, [(i, i ^ mask) for i in range(count)])


def cost(flops, nbytes):
    return pl.CostEstimate(flops=int(flops), bytes_accessed=int(nbytes), transcendentals=0)


def mirrored(value, bits):
    result = value * 0
    for low in range(bits):
        result = result | (((value >> low) & 1) << (bits - 1 - low))
    return result


def masks(count):
    return list(range(count - 1, 0, -1))


def lanes(start):
    return pl.multiple_of(start, 128)


def window(shape, offsets):
    return pl.BlockSpec(tuple(pl.Element(size) for size in shape), offsets)


def params():
    return pltpu.CompilerParams(vmem_limit_bytes=GRANT)


def block_of(rows, unit, first, pick):
    def offsets(i, ids_ref):
        return 0, pl.multiple_of(ids_ref[pick] * rows, rows), lanes(first + i * unit)

    return window((2, rows, unit), offsets)


def resident():
    return pl.BlockSpec(memory_space=pltpu.VMEM)


def fetch(echoes_ref, ids_ref, pick, first, out_ref, sem):
    rows, unit = out_ref.shape[1:]
    start = pl.multiple_of(ids_ref[pick] * rows, rows)
    source = echoes_ref.at[:, pl.ds(start, rows), pl.ds(first, unit)]
    return pltpu.make_async_copy(source, out_ref, sem)


def cut_kernel(chosen, first, ids_ref, echoes_ref, *refs):
    outs, sems = refs[:-1], refs[-1]
    copies = [
        fetch(echoes_ref, ids_ref, k, first, outs[place], sems.at[place])
        for place, k in enumerate(chosen)
    ]
    for copy in copies:
        copy.start()
    for copy in copies:
        copy.wait()


def cut_blocks(echoes, ids, chosen, first, unit, rows):
    return pl.pallas_call(
        functools.partial(cut_kernel, chosen, first),
        out_shape=[jax.ShapeDtypeStruct((2, rows, unit), echoes.dtype)] * len(chosen),
        grid_spec=pltpu.PrefetchScalarGridSpec(
            num_scalar_prefetch=1,
            grid=(1,),
            in_specs=[pl.BlockSpec(memory_space=pl.ANY)],
            out_specs=[resident()] * len(chosen),
            scratch_shapes=[pltpu.SemaphoreType.DMA((len(chosen),))],
        ),
        compiler_params=params(),
        cost_estimate=cost(0, 8 * len(chosen) * rows * unit),
        name="cut_blocks",
    )(ids, echoes)


def lend_kernel(count, first, ids_ref, echoes_ref, out_ref, sems):
    copies = [
        fetch(echoes_ref, ids_ref, 2 * d + 1, first, out_ref.at[d], sems.at[d])
        for d in range(count)
    ]
    for copy in copies:
        copy.start()
    for copy in copies:
        copy.wait()


def lend_blocks(echoes, ids, first, unit, rows):
    count = lax.axis_size("tile") // 2
    return pl.pallas_call(
        functools.partial(lend_kernel, count, first),
        out_shape=jax.ShapeDtypeStruct((count, 2, rows, unit), echoes.dtype),
        grid_spec=pltpu.PrefetchScalarGridSpec(
            num_scalar_prefetch=1,
            grid=(1,),
            in_specs=[pl.BlockSpec(memory_space=pl.ANY)],
            out_specs=resident(),
            scratch_shapes=[pltpu.SemaphoreType.DMA((count,))],
        ),
        compiler_params=params(),
        cost_estimate=cost(0, 8 * count * rows * unit),
        name="lend_blocks",
    )(ids, echoes)


def join_kernel(chosen, first, start, ids_ref, echoes_ref, lent_ref, *refs):
    outs, sems = refs[:-1], refs[-1]
    copies = [
        fetch(echoes_ref, ids_ref, 2 * d, first, outs[place].at[0], sems.at[place])
        for place, d in enumerate(chosen)
    ]
    for copy in copies:
        copy.start()
    for place, d in enumerate(chosen):
        outs[place][1] = lent_ref[d, :, :, start : start + outs[place].shape[3]]
    for copy in copies:
        copy.wait()


def join_blocks(echoes, lent, ids, first, behind, unit, rows):
    chosen = masks(lax.axis_size("tile") // 2)
    return pl.pallas_call(
        functools.partial(join_kernel, chosen, first, first - behind),
        out_shape=[jax.ShapeDtypeStruct((2, 2, rows, unit), echoes.dtype)] * len(chosen),
        grid_spec=pltpu.PrefetchScalarGridSpec(
            num_scalar_prefetch=1,
            grid=(1,),
            in_specs=[pl.BlockSpec(memory_space=pl.ANY), resident()],
            out_specs=[resident()] * len(chosen),
            scratch_shapes=[pltpu.SemaphoreType.DMA((len(chosen),))],
        ),
        compiler_params=params(),
        cost_estimate=cost(0, 16 * len(chosen) * rows * unit),
        name="join_blocks",
    )(ids, echoes, lent)


def steer_kernel(count, subs, start, ids_ref, weights_ref, own_ref, *refs):
    outs, held = refs[-1 - subs : -1], refs[-1]
    weights = weights_ref[...]
    unit = own_ref.shape[2]
    for k in range(count):
        if k == 0:
            block = own_ref[...]
        elif start is None:
            block = refs[count - 1 - k][...]
        elif k == 1:
            block = refs[0][0, :, :, start : start + unit]
        else:
            block = refs[count // 2 - k // 2][k % 2]
        block = block.reshape(block.shape[0] * block.shape[1], unit)
        beams = jnp.dot(weights, block, preferred_element_type=jnp.float32)
        held[ids_ref[count + k], ids_ref[2 * count + k]] = beams.astype(held.dtype)
    for r in range(subs):
        outs[r][...] = held[r]


def steer_blocks(echoes, lent, arrived, weights, ids, first, behind, unit, rows, after):
    count, subs = lax.axis_size("tile"), lax.axis_size("sub")
    pieces = count // subs
    height = weights.shape[0]
    operands = ([] if lent is None else [lent]) + arrived
    shape = (pieces, height, unit)
    return pl.pallas_call(
        functools.partial(steer_kernel, count, subs, None if lent is None else first - behind),
        out_shape=[jax.ShapeDtypeStruct(shape, echoes.dtype)] * subs,
        grid_spec=pltpu.PrefetchScalarGridSpec(
            num_scalar_prefetch=1,
            grid=(1,),
            in_specs=[resident(), block_of(rows, unit, first, 0)]
            + [resident()] * len(operands)
            + [pl.BlockSpec(memory_space=pl.ANY)] * len(after),
            out_specs=[resident()] * subs,
            scratch_shapes=[pltpu.VMEM((subs,) + shape, echoes.dtype)],
        ),
        compiler_params=params(),
        cost_estimate=cost(2 * count * height * height * unit, 4 * count * height * unit),
        name="steer_blocks",
    )(ids, weights, echoes, *operands, *after)


def turned(block, cosine, sine):
    half = block.shape[0] // 2
    real = block[:half].astype(jnp.float32)
    imag = block[half:].astype(jnp.float32)
    return jnp.concatenate(
        [
            (real * cosine - imag * sine).astype(jnp.bfloat16),
            (real * sine + imag * cosine).astype(jnp.bfloat16),
        ],
        axis=0,
    )


def merge_kernel(levels, subs, given, final, first, ids_ref, *refs):
    phases_ref = refs[subs]
    mats = refs[subs + 1 : subs + 1 + levels]
    map_ref = refs[subs + 1 + levels]
    rest = refs[subs + 2 + levels : -2]
    held, sems = refs[-2:]
    pieces, local = map_ref.shape[:2]
    unit = held.shape[0] // pieces
    copies = [
        pltpu.make_async_copy(
            map_ref.at[e, pl.ds(first, unit)], held.at[pl.ds(e * unit, unit)], sems.at[e]
        )
        for e in range(pieces)
    ]
    for copy in copies:
        copy.start()
    phases = jnp.concatenate(
        [phases_ref[:, e * local + first : e * local + first + unit] for e in range(pieces)], axis=1
    )
    cosines, sines = jnp.cos(phases), jnp.sin(phases)
    sources = [jnp.concatenate([ref[e] for e in range(pieces)], axis=1) for ref in refs[:subs]]
    row = 0
    for level in range(levels):
        merged = []
        for h in range(len(sources) // 2):
            children = [
                turned(
                    sources[2 * h + c],
                    cosines[row + c : row + c + 1],
                    sines[row + c : row + c + 1],
                )
                for c in range(2)
            ]
            row += 2
            product = jnp.dot(
                mats[level][h],
                jnp.concatenate(children, axis=0),
                preferred_element_type=jnp.float32,
            )
            merged.append(product.astype(jnp.bfloat16))
        sources = merged
    for copy in copies:
        copy.wait()
    if given:
        before, rest = rest[0], rest[1:]
    columns = held.shape[1]
    width = columns // subs
    for r in range(subs):
        start = r * width
        if final:
            start = pl.multiple_of(ids_ref[r] * width, width)
        part = pl.ds(start, width)
        share = jnp.dot(sources[0], held[:, part], preferred_element_type=jnp.float32)
        if given:
            share = before[:, part] + share
        if final:
            strips = len(rest) // subs
            for strip in range(strips):
                out = rest[strip * subs + r]
                span = out.shape[1]
                out[...] = share[:, strip * span : (strip + 1) * span].astype(out.dtype)
        else:
            rest[0][:, part] = share


def merge_blocks(sources, phases, mats, range_map, ids, before, final, first):
    subs, levels = len(sources), len(mats)
    pieces, height, unit = sources[0].shape
    columns = range_map.shape[2]
    beams = mats[-1].shape[1]
    given = before is not None
    operands = [*sources, phases, *mats]
    in_specs = [resident()] * len(operands) + [pl.BlockSpec(memory_space=pl.ANY)]
    operands = [ids, *operands, range_map]
    aliases = {}
    if given:
        in_specs.append(resident())
        operands.append(before)
    if final:
        strips = max(1, columns // subs // 128)
        width = columns // subs // strips
        out_shape = [jax.ShapeDtypeStruct((beams, width), jnp.bfloat16)] * (subs * strips)
        out_specs = [resident()] * (subs * strips)
    else:
        out_shape = jax.ShapeDtypeStruct((beams, columns), jnp.float32)
        out_specs = resident()
        if given:
            aliases = {len(operands) - 1: 0}
    gates = pieces * unit
    flops = sum(2 * mat.size for mat in mats) * gates + 2 * beams * columns * gates
    return pl.pallas_call(
        functools.partial(merge_kernel, levels, subs, given, final, first),
        out_shape=out_shape,
        grid_spec=pltpu.PrefetchScalarGridSpec(
            num_scalar_prefetch=1,
            grid=(1,),
            in_specs=in_specs,
            out_specs=out_specs,
            scratch_shapes=[
                pltpu.VMEM((gates, columns), range_map.dtype),
                pltpu.SemaphoreType.DMA((pieces,)),
            ],
        ),
        input_output_aliases=aliases,
        compiler_params=params(),
        cost_estimate=cost(flops, 2 * columns * gates + 2 * subs * height * gates),
        name="merge_blocks",
    )(*operands)


def beam_kernel(subs, foot, ids_ref, *refs):
    pieces = refs[:subs]
    near_ref, far_ref, keep_ref, send_ref, held = refs[subs:]
    step = pl.program_id(0)
    count = pl.num_programs(0)

    @pl.when(step == 0)
    def _():
        total = pieces[0][...].astype(jnp.float32)
        for piece in pieces[1:]:
            total = total + piece[...].astype(jnp.float32)
        held[...] = total.astype(held.dtype)

    planes = keep_ref.shape[1]
    depth = held.shape[0] // planes
    for side, map_ref, out_ref in ((0, near_ref, keep_ref), (1, far_ref, send_ref)):
        tile = ids_ref[2 * step + side]
        covered = ids_ref[2 * count] == tile
        for entry in range(1, foot):
            covered = jnp.logical_or(covered, ids_ref[2 * count + entry] == tile)

        @pl.when(covered)
        def _():
            for plane in range(planes):
                out_ref[step, plane] = jnp.dot(
                    map_ref[0],
                    held[plane * depth : (plane + 1) * depth],
                    preferred_element_type=jnp.float32,
                ).astype(out_ref.dtype)

        @pl.when(jnp.logical_not(covered))
        def _():
            out_ref[step] = jnp.zeros(out_ref.shape[1:], out_ref.dtype)


def beam_blocks(pieces, beam_map, ids):
    tiles, rows, depth = beam_map.shape
    count = tiles // 2
    height, width = pieces[0].shape
    planes = height // depth
    shape = (count, planes, rows, width)

    def pick(side):
        return pl.BlockSpec((1, rows, depth), lambda i, ids_ref: (ids_ref[2 * i + side], 0, 0))

    return pl.pallas_call(
        functools.partial(beam_kernel, len(pieces), ids.shape[0] - tiles),
        out_shape=[
            jax.ShapeDtypeStruct(shape, jnp.float32),
            jax.ShapeDtypeStruct(shape, jnp.bfloat16),
        ],
        grid_spec=pltpu.PrefetchScalarGridSpec(
            num_scalar_prefetch=1,
            grid=(count,),
            in_specs=[resident()] * len(pieces)
            + [pick(0), pick(1)],
            out_specs=[resident(), resident()],
            scratch_shapes=[pltpu.VMEM((height, width), jnp.bfloat16)],
        ),
        compiler_params=params(),
        cost_estimate=cost(2 * tiles * rows * depth * planes * width, 2 * beam_map.size),
        name="beam_blocks",
    )(ids, *pieces, beam_map, beam_map)


def own_first(pair, upper):
    return jnp.stack([jnp.where(upper == 1, pair[1 - c], pair[c]) for c in range(2)])


def angle_packets(angles, gates, base, piece):
    sub_index, subs = lax.axis_index("sub"), lax.axis_size("sub")
    levels = subs.bit_length() - 1
    packets = []
    for level in range(levels):
        beams = base << level
        higher = sub_index >> (level + 1)
        for h in range(subs >> (level + 1)):
            start = 2 * beams
            for bit in range(levels - level - 1):
                start = start + (((higher ^ h) >> bit) & 1) * (gates >> (level + 2 + bit))
            packet = jnp.concatenate(
                [
                    angles[level, :, : 2 * beams],
                    lax.dynamic_slice_in_dim(angles[level], start, piece, 1),
                ],
                axis=1,
            )
            packets.append(swap(packet, "sub", h << (level + 1)) if h else packet)
    return packets


def merge_tables(interp, packets, base):
    sub_index, subs = lax.axis_index("sub"), lax.axis_size("sub")
    levels = subs.bit_length() - 1
    mats, rows, offset = [], [], 0
    packets = list(packets)
    for level in range(levels):
        beams = base << level
        upper = (sub_index >> level) & 1
        size = 4 * beams * beams
        weights = interp[offset : offset + size].reshape(2, 2 * beams, beams).astype(jnp.float32)
        offset += size
        weights = own_first(weights, upper) * (2.0 * beams) ** -0.5
        group = []
        for _ in range(subs >> (level + 1)):
            packet = own_first(packets.pop(0), upper)
            cosine, sine = jnp.cos(packet[:, : 2 * beams]), jnp.sin(packet[:, : 2 * beams])
            real = cosine[:, :, None] * weights
            imag = sine[:, :, None] * weights
            group.append(
                jnp.concatenate(
                    [
                        jnp.concatenate([real[0], -imag[0], real[1], -imag[1]], axis=1),
                        jnp.concatenate([imag[0], real[0], imag[1], real[1]], axis=1),
                    ],
                    axis=0,
                ).astype(jnp.bfloat16)
            )
            rows.append(packet[:, 2 * beams :])
        mats.append(jnp.stack(group))
    missing = -2 * len(rows) % 8
    if missing:
        rows.append(jnp.zeros((missing, rows[0].shape[1]), jnp.float32))
    return mats, jnp.concatenate(rows)


def on_device(echoes, steering, interp, angles, range_map, beam_map, footprint):
    tiles, subs = lax.axis_size("tile"), lax.axis_size("sub")
    tile_index, sub_index = lax.axis_index("tile"), lax.axis_index("sub")
    pieces = tiles // subs
    local = echoes.shape[2]
    echoes = pltpu.with_memory_space_constraint(echoes, pltpu.HBM)
    base = steering.shape[1]
    bits = subs.bit_length() - 1

    sources = [tile_index ^ k for k in range(tiles)]
    slots = [sub_index ^ mirrored(source // pieces, bits) for source in sources]
    spots = [source % pieces for source in sources]
    ids = jnp.stack(sources + slots + spots).astype(jnp.int32)
    column_ids = jnp.stack([sub_index ^ r for r in range(subs)]).astype(jnp.int32)

    ends = [int(share * local) // 128 * 128 for share in SHARES]
    stretches = [(one, two - one) for one, two in zip(ends, ends[1:])]
    opening = stretches[0][1]

    cuts = []
    for chosen in (masks(tiles)[:2], masks(tiles)[2:]):
        cuts += cut_blocks(echoes, ids, chosen, 0, opening, base)
    arrived = [[swap(cut, "tile", k) for cut, k in zip(cuts, masks(tiles))]]
    lent = lend_blocks(echoes, ids, opening, local - opening, base)
    lent = swap(lent, "tile", 1)
    steer = jnp.concatenate(
        [
            jnp.concatenate([steering[0], -steering[1]], axis=1),
            jnp.concatenate([steering[1], steering[0]], axis=1),
        ],
        axis=0,
    )
    angles, cuts = lax.optimization_barrier((angles, cuts))
    packets = angle_packets(angles[0, 0], local * tiles, base, local * pieces)
    for part_id, (first, length) in list(enumerate(stretches))[1:]:
        joined = join_blocks(echoes, lent, ids, first, opening, length, base)
        arrived.append([swap(part, "tile", 2 * d) for part, d in zip(joined, masks(tiles // 2))])
        if part_id == 1:
            interp, packets, _ = lax.optimization_barrier((interp, packets, joined[-1]))
            mats, phases = merge_tables(interp, packets, base)

    map_rows = range_map[0].reshape(pieces, local, range_map.shape[2])
    map_rows = pltpu.with_memory_space_constraint(map_rows, pltpu.HBM)

    totals = [None, None]
    for (first, length), blocks in zip(stretches, arrived):
        parts = steer_blocks(
            echoes,
            lent if first else None,
            blocks,
            steer,
            ids,
            first,
            opening,
            length,
            base,
            [] if totals[-2] is None or first + length == local else [totals[-2]],
        )
        parts = [parts[0]] + [swap(parts[r], "sub", r) for r in range(1, subs)]
        final = first + length == local
        merged = merge_blocks(parts, phases, mats, map_rows, column_ids, totals[-1], final, first)
        totals.append(merged)
    total = totals[-1]

    beam_ids = jnp.concatenate([jnp.stack(sources).astype(jnp.int32), footprint[0]])
    strips = []
    for strip in range(len(total) // subs):
        mine = total[strip * subs : (strip + 1) * subs]
        strips.append([mine[0]] + [swap(mine[r], "sub", r) for r in range(1, subs)])
    images = []
    for quarters in strips:
        keep, send = beam_blocks(quarters, beam_map[0], beam_ids)
        other = swap(send, "tile", 1)
        image = keep[0] + other[0].astype(jnp.float32)
        for d in masks(tiles // 2):
            part = (keep[d] + other[d].astype(jnp.float32)).astype(jnp.bfloat16)
            part = swap(part, "tile", 2 * d)
            image = image + part.astype(jnp.float32)
        images.append(image)
    return jnp.concatenate(images, axis=2)


def solution(mesh):
    placed = (
        P(None, "sub", "tile"),
        P(None, ("sub", "tile"), None),
        P(),
        P("tile", "sub", None, None, None),
        P("tile", "sub", None),
        P("tile", None, None, None),
        P("tile", None),
    )

    return jax.shard_map(
        on_device, mesh=mesh, in_specs=placed, out_specs=P(None, "tile", "sub"), check_vma=False
    )
```

profile of v0, /device:TPU:0, one launch (start us, length us, event | category | flops | bytes accessed | tf_op | source)
XLA Modules:
  0.0 197.0 jit_solution(5302506639208379795)
XLA Ops:
  0.1 2.3 %cut_blocks.2 = (bf16[2,64,896]{2,1,0:T(8,128)(2,1)S(1)}, bf16[2,64,896]{2,1,0:T(8,128)(2,1)}) custom-call(s32[24]{0:T(128)S(1)} %stack.158.ids_ref, bf16[2,512,2048]{2,1,0:T(8,128)(2,1)} %own_ref.7), custom_call_target="tpu_custom_call" | custom-call | bytes 917504 | tf_op jit(solution)/shard_map/cut_blocks/pallas_call | solution.py:78
  2.4 4.6 %collective-permute-start.11 = (bf16[2,64,896]{2,1,0:T(8,128)(2,1)S(1)}, bf16[2,64,896]{2,1,0:T(8,128)(2,1)S(1)}, u32[]{:S(2)}, u32[]{:S(2)}) collective-permute-start(bf16[2,64,896]{2,1,0:T(8,128)(2,1)S(1)} %get-tuple-element.61), channel_id=1, source_target_pairs={{0,7},{1,6},{2,5},{3,4},{4,3},{5,2},{6,1},{7,0},{8,15},{9,14},{10,... | collective-permute-start | bytes 688136 | tf_op jit(solution)/shard_map/ppermute | solution.py:17
  7.6 2.7 %cut_blocks.3 = (bf16[2,64,896]{2,1,0:T(8,128)(2,1)}, bf16[2,64,896]{2,1,0:T(8,128)(2,1)}, bf16[2,64,896]{2,1,0:T(8,128)(2,1)S(1)}, bf16[2,64,896]{2,1,0:T(8,128)(2,1)S(1)}, bf16[2,64,896]{2,1,0:T(8,128)(2,1)S(1)}) custom-call(s32[24]{0:T(128)S(1)} %stack.158.ids_ref, bf16[2,512,2048]{2,1,0:T(8,128)(2,1)} %own_ref.7), custom_call_target="tpu_custom_call" | custom-call | bytes 2293760 | tf_op jit(solution)/shard_map/cut_blocks/pallas_call | solution.py:78
  12.8 2.2 %collective-permute-start.14 = (bf16[2,64,896]{2,1,0:T(8,128)(2,1)}, bf16[2,64,896]{2,1,0:T(8,128)(2,1)S(1)}, u32[]{:S(2)}, u32[]{:S(2)}) collective-permute-start(bf16[2,64,896]{2,1,0:T(8,128)(2,1)} %get-tuple-element.64), channel_id=1, source_target_pairs={{0,4},{1,5},{2,6},{3,7},{4,0},{5,1},{6,2},{7,3},{8,12},{9,13},{10,... | collective-permute-start | bytes 688136 | tf_op jit(solution)/shard_map/ppermute | solution.py:17
  24.3 8.4 %collective-permute-start.15 = (bf16[2,64,896]{2,1,0:T(8,128)(2,1)}, bf16[2,64,896]{2,1,0:T(8,128)(2,1)S(1)}, u32[]{:S(2)}, u32[]{:S(2)}) collective-permute-start(bf16[2,64,896]{2,1,0:T(8,128)(2,1)} %copy-done.7), channel_id=1, source_target_pairs={{0,3},{1,2},{2,1},{3,0},{4,7},{5,6},{6,5},{7,4},{8,11},{9,10},{10,... | collective-permute-start | bytes 688136 | tf_op jit(solution)/shard_map/ppermute | solution.py:17
  32.7 5.5 %collective-permute-start.16 = (bf16[2,64,896]{2,1,0:T(8,128)(2,1)}, bf16[2,64,896]{2,1,0:T(8,128)(2,1)}, u32[]{:S(2)}, u32[]{:S(2)}) collective-permute-start(bf16[2,64,896]{2,1,0:T(8,128)(2,1)} %copy-done.6), channel_id=1, source_target_pairs={{0,2},{1,3},{2,0},{3,1},{4,6},{5,7},{6,4},{7,5},{8,10},{9,11},{10,... | collective-permute-start | bytes 688136 | tf_op jit(solution)/shard_map/ppermute | solution.py:17
  38.1 4.2 %collective-permute-done.13.refs_2_ = bf16[2,64,896]{2,1,0:T(8,128)(2,1)S(1)} collective-permute-done((bf16[2,64,896]{2,1,0:T(8,128)(2,1)}, bf16[2,64,896]{2,1,0:T(8,128)(2,1)S(1)}, u32[]{:S(2)}, u32[]{:S(2)}) %collective-permute-start.13) | collective-permute-done | bytes 229408 | tf_op jit(solution)/shard_map/ppermute | solution.py:17
  44.6 2.8 %collective-permute-done.14.refs_3_ = bf16[2,64,896]{2,1,0:T(8,128)(2,1)S(1)} collective-permute-done((bf16[2,64,896]{2,1,0:T(8,128)(2,1)}, bf16[2,64,896]{2,1,0:T(8,128)(2,1)S(1)}, u32[]{:S(2)}, u32[]{:S(2)}) %collective-permute-start.14) | collective-permute-done | bytes 229408 | tf_op jit(solution)/shard_map/ppermute | solution.py:17
  50.4 3.5 %collective-permute-done.16.refs_5_ = bf16[2,64,896]{2,1,0:T(8,128)(2,1)} collective-permute-done((bf16[2,64,896]{2,1,0:T(8,128)(2,1)}, bf16[2,64,896]{2,1,0:T(8,128)(2,1)}, u32[]{:S(2)}, u32[]{:S(2)}) %collective-permute-start.16) | collective-permute-done | bytes 229408 | tf_op jit(solution)/shard_map/ppermute | solution.py:17
  55.8 3.5 %steer_blocks.5 = (bf16[2,128,896]{2,1,0:T(8,128)(2,1)S(1)}, bf16[2,128,896]{2,1,0:T(8,128)(2,1)}, bf16[2,128,896]{2,1,0:T(8,128)(2,1)}, bf16[2,128,896]{2,1,0:T(8,128)(2,1)}) custom-call(s32[24]{0:T(128)S(1)} %stack.158.ids_ref, bf16[128,128]{1,0:T(8,128)(2,1)S(1)} %maximum_maximum_fusion.2.weights_ref, bf16[2,512,2048]{2,1,0:T(8,128)(2,1)} %own_ref.7, ...), custom_call_target="tpu_custom_call" | custom-call | flops 234881024 | bytes 3670016 | tf_op jit(solution)/shard_map/steer_blocks/pallas_call | solution.py:181
  66.4 2.7 %collective-permute-start.24 = (bf16[2,2,64,384]{3,2,1,0:T(8,128)(2,1)S(1)}, bf16[2,2,64,384]{3,2,1,0:T(8,128)(2,1)S(1)}, u32[]{:S(2)}, u32[]{:S(2)}) collective-permute-start(bf16[2,2,64,384]{3,2,1,0:T(8,128)(2,1)S(1)} %get-tuple-element.85), channel_id=1, source_target_pairs={{0,6},{1,7},{2,4},{3,5},{4,2},{5,3},{6,0},{7,1},{8,14},{9,15},{10,... | collective-permute-start | bytes 589832 | tf_op jit(solution)/shard_map/ppermute | solution.py:17
  72.8 3.9 %collective-permute-done.24.refs_1_ = bf16[2,2,64,384]{3,2,1,0:T(8,128)(2,1)S(1)} collective-permute-done((bf16[2,2,64,384]{3,2,1,0:T(8,128)(2,1)S(1)}, bf16[2,2,64,384]{3,2,1,0:T(8,128)(2,1)S(1)}, u32[]{:S(2)}, u32[]{:S(2)}) %collective-permute-start.24) | collective-permute-done | bytes 196640 | tf_op jit(solution)/shard_map/ppermute | solution.py:17
  76.8 2.3 %collective-permute-start.25 = (bf16[2,2,64,384]{3,2,1,0:T(8,128)(2,1)S(1)}, bf16[2,2,64,384]{3,2,1,0:T(8,128)(2,1)S(1)}, u32[]{:S(2)}, u32[]{:S(2)}) collective-permute-start(bf16[2,2,64,384]{3,2,1,0:T(8,128)(2,1)S(1)} %get-tuple-element.86), channel_id=1, source_target_pairs={{0,4},{1,5},{2,6},{3,7},{4,0},{5,1},{6,2},{7,3},{8,12},{9,13},{10,... | collective-permute-start | bytes 589832 | tf_op jit(solution)/shard_map/ppermute | solution.py:17
  79.3 7.8 %collective-permute-done.25.refs_2_ = bf16[2,2,64,384]{3,2,1,0:T(8,128)(2,1)S(1)} collective-permute-done((bf16[2,2,64,384]{3,2,1,0:T(8,128)(2,1)S(1)}, bf16[2,2,64,384]{3,2,1,0:T(8,128)(2,1)S(1)}, u32[]{:S(2)}, u32[]{:S(2)}) %collective-permute-start.25) | collective-permute-done | bytes 196640 | tf_op jit(solution)/shard_map/ppermute | solution.py:17
  90.4 3.0 %collective-permute-start.10 = (bf16[2,2,64,384]{3,2,1,0:T(8,128)(2,1)S(1)}, bf16[2,2,64,384]{3,2,1,0:T(8,128)(2,1)S(1)}, u32[]{:S(2)}, u32[]{:S(2)}) collective-permute-start(bf16[2,2,64,384]{3,2,1,0:T(8,128)(2,1)S(1)} %get-tuple-element.76), channel_id=1, source_target_pairs={{0,2},{1,3},{2,0},{3,1},{4,6},{5,7},{6,4},{7,5},{8,10},{9,11},{10,... | collective-permute-start | bytes 589832 | tf_op jit(solution)/shard_map/ppermute | solution.py:17
  96.7 6.4 %collective-permute-start.3 = (bf16[2,2,64,384]{3,2,1,0:T(8,128)(2,1)S(1)}, bf16[2,2,64,384]{3,2,1,0:T(8,128)(2,1)S(1)}, u32[]{:S(2)}, u32[]{:S(2)}) collective-permute-start(bf16[2,2,64,384]{3,2,1,0:T(8,128)(2,1)S(1)} %get-tuple-element.56), channel_id=1, source_target_pairs={{0,2},{1,3},{2,0},{3,1},{4,6},{5,7},{6,4},{7,5},{8,10},{9,11},{10,... | collective-permute-start | bytes 589832 | tf_op jit(solution)/shard_map/ppermute | solution.py:17
  103.1 10.4 %collective-permute-done.9.refs_2_ = bf16[2,2,64,384]{3,2,1,0:T(8,128)(2,1)S(1)} collective-permute-done((bf16[2,2,64,384]{3,2,1,0:T(8,128)(2,1)S(1)}, bf16[2,2,64,384]{3,2,1,0:T(8,128)(2,1)S(1)}, u32[]{:S(2)}, u32[]{:S(2)}) %collective-permute-start.9) | collective-permute-done | bytes 196640 | tf_op jit(solution)/shard_map/ppermute | solution.py:17
  115.0 6.4 %merge_blocks.4.refs_4_.refs_8_ = f32[512,1024]{1,0:T(8,128)S(1)} custom-call(s32[4]{0:T(128)S(1)} %pad_add_fusion.ids_ref, bf16[2,128,896]{2,1,0:T(8,128)(2,1)S(1)} %get-tuple-element.77.refs_0_, bf16[2,128,896]{2,1,0:T(8,128)(2,1)S(1)} %collective-permute-done.18.refs_1_, bf16[2,128,896]{2,1,0:T(8,128)(2,1)} %collective-permute-done.19.refs_2_, ...), custom_call_target="tpu_custom_call" | custom-call | flops 3288334336 | bytes 5505024 | tf_op jit(solution)/shard_map/merge_blocks/pallas_call | solution.py:302
  130.8 4.8 %collective-permute-done.28.refs_2_ = bf16[2,128,384]{2,1,0:T(8,128)(2,1)S(1)} collective-permute-done((bf16[2,128,384]{2,1,0:T(8,128)(2,1)S(1)}, bf16[2,128,384]{2,1,0:T(8,128)(2,1)S(1)}, u32[]{:S(2)}, u32[]{:S(2)}) %collective-permute-start.28) | collective-permute-done | bytes 196640 | tf_op jit(solution)/shard_map/ppermute | solution.py:17
  135.5 2.1 %collective-permute-start.5 = (bf16[2,128,384]{2,1,0:T(8,128)(2,1)S(1)}, bf16[2,128,384]{2,1,0:T(8,128)(2,1)S(1)}, u32[]{:S(2)}, u32[]{:S(2)}) collective-permute-start(bf16[2,128,384]{2,1,0:T(8,128)(2,1)S(1)} %get-tuple-element.59), channel_id=1, source_target_pairs={{0,16},{8,24},{16,0},{24,8},{1,17},{9,25},{17,1},{25,9},{2,18},{10... | collective-permute-start | bytes 589832 | tf_op jit(solution)/shard_map/ppermute | solution.py:17
  139.0 3.8 %merge_blocks.5.refs_8_ = f32[512,1024]{1,0:T(8,128)S(1)} custom-call(s32[4]{0:T(128)S(1)} %pad_add_fusion.ids_ref, bf16[2,128,384]{2,1,0:T(8,128)(2,1)S(1)} %get-tuple-element.87.refs_0_, bf16[2,128,384]{2,1,0:T(8,128)(2,1)S(1)} %collective-permute-done.27.refs_1_, ...), custom_call_target="tpu_custom_call", output_to_operand_aliasing={{}: (9, {})} | custom-call | flops 1409286144 | bytes 2359296 | tf_op jit(solution)/shard_map/merge_blocks/pallas_call | solution.py:302
  142.8 3.6 %merge_blocks.6.refs_8_ = f32[512,1024]{1,0:T(8,128)S(1)} custom-call(s32[4]{0:T(128)S(1)} %pad_add_fusion.ids_ref, bf16[2,128,384]{2,1,0:T(8,128)(2,1)S(1)} %get-tuple-element.81.refs_0_, bf16[2,128,384]{2,1,0:T(8,128)(2,1)S(1)} %collective-permute-done.21.refs_1_, ...), custom_call_target="tpu_custom_call", output_to_operand_aliasing={{}: (9, {})} | custom-call | flops 1409286144 | bytes 2359296 | tf_op jit(solution)/shard_map/merge_blocks/pallas_call | solution.py:302
  146.5 2.9 %merge_blocks.7 = (bf16[512,128]{1,0:T(8,128)(2,1)S(1)}, bf16[512,128]{1,0:T(8,128)(2,1)S(1)}, bf16[512,128]{1,0:T(8,128)(2,1)S(1)}, bf16[512,128]{1,0:T(8,128)(...) custom-call(s32[4]{0:T(128)S(1)} %pad_add_fusion.ids_ref, ...), custom_call_target="tpu_custom_call" | custom-call | flops 1409286144 | bytes 2359296 | tf_op jit(solution)/shard_map/merge_blocks/pallas_call | solution.py:302
  149.6 2.0 collective-permute-start.38
  155.4 1.9 collective-permute-done.39.refs_3_
  162.7 2.9 %collective-permute-done.30.refs_1_ = bf16[512,128]{1,0:T(8,128)(2,1)S(1)} collective-permute-done((bf16[512,128]{1,0:T(8,128)(2,1)S(1)}, bf16[512,128]{1,0:T(8,128)(2,1)S(1)}, u32[]{:S(2)}, u32[]{:S(2)}) %collective-permute-start.30) | collective-permute-done | bytes 131104 | tf_op jit(solution)/shard_map/ppermute | solution.py:17
  165.6 3.0 %collective-permute-done.31.refs_2_ = bf16[512,128]{1,0:T(8,128)(2,1)S(1)} collective-permute-done((bf16[512,128]{1,0:T(8,128)(2,1)S(1)}, bf16[512,128]{1,0:T(8,128)(2,1)S(1)}, u32[]{:S(2)}, u32[]{:S(2)}) %collective-permute-start.31) | collective-permute-done | bytes 131104 | tf_op jit(solution)/shard_map/ppermute | solution.py:17
  170.5 2.7 %collective-permute-start.41 = (bf16[2,256,128]{2,1,0:T(8,128)(2,1)S(1)}, bf16[2,256,128]{2,1,0:T(8,128)(2,1)S(1)}, u32[]{:S(2)}, u32[]{:S(2)}) collective-permute-start(bf16[2,256,128]{2,1,0:T(8,128)(2,1)S(1)} %get-tuple-element.112), channel_id=1, source_target_pairs={{0,6},{1,7},{2,4},{3,5},{4,2},{5,3},{6,0},{7,1},{8,14},{9,15},{10,... | collective-permute-start | bytes 393224 | tf_op jit(solution)/shard_map/ppermute | solution.py:17
  175.0 2.7 %collective-permute-start.34 = (bf16[2,256,128]{2,1,0:T(8,128)(2,1)S(1)}, bf16[2,256,128]{2,1,0:T(8,128)(2,1)S(1)}, u32[]{:S(2)}, u32[]{:S(2)}) collective-permute-start(bf16[2,256,128]{2,1,0:T(8,128)(2,1)S(1)} %get-tuple-element.109), channel_id=1, source_target_pairs={{0,6},{1,7},{2,4},{3,5},{4,2},{5,3},{6,0},{7,1},{8,14},{9,15},{10,... | collective-permute-start | bytes 393224 | tf_op jit(solution)/shard_map/ppermute | solution.py:17
  179.5 3.7 %collective-permute-done.43 = bf16[2,256,128]{2,1,0:T(8,128)(2,1)S(1)} collective-permute-done((bf16[2,256,128]{2,1,0:T(8,128)(2,1)S(1)}, bf16[2,256,128]{2,1,0:T(8,128)(2,1)S(1)}, u32[]{:S(2)}, u32[]{:S(2)}) %collective-permute-start.43) | collective-permute-done | bytes 131104 | tf_op jit(solution)/shard_map/ppermute | solution.py:17
  183.2 5.0 %collective-permute-done.42 = bf16[2,256,128]{2,1,0:T(8,128)(2,1)S(1)} collective-permute-done((bf16[2,256,128]{2,1,0:T(8,128)(2,1)S(1)}, bf16[2,256,128]{2,1,0:T(8,128)(2,1)S(1)}, u32[]{:S(2)}, u32[]{:S(2)}) %collective-permute-start.42) | collective-permute-done | bytes 131104 | tf_op jit(solution)/shard_map/ppermute | solution.py:17
  189.5 6.5 %collective-permute-done.35 = bf16[2,256,128]{2,1,0:T(8,128)(2,1)S(1)} collective-permute-done((bf16[2,256,128]{2,1,0:T(8,128)(2,1)S(1)}, bf16[2,256,128]{2,1,0:T(8,128)(2,1)S(1)}, u32[]{:S(2)}, u32[]{:S(2)}) %collective-permute-start.35) | collective-permute-done | bytes 131104 | tf_op jit(solution)/shard_map/ppermute | solution.py:17
  (153 shorter events, 66.6 us)
Async XLA Ops:
  2.4 21.9 %collective-permute-start.11 = (bf16[2,64,896]{2,1,0:T(8,128)(2,1)S(1)}, bf16[2,64,896]{2,1,0:T(8,128)(2,1)S(1)}, u32[]{:S(2)}, u32[]{:S(2)}) collective-permute-start(bf16[2,64,896]{2,1,0:T(8,128)(2,1)S(1)} %get-tuple-element.61), channel_id=1, source_target_pairs={{0,7},{1,6},{2,5},{3,4},{4,3},{5,2},{6,1},{7,0},{8,15},{9,14},{10,... | collective-permute-start | bytes 688136 | tf_op jit(solution)/shard_map/ppermute | solution.py:17
  7.0 25.7 %collective-permute-start.12 = (bf16[2,64,896]{2,1,0:T(8,128)(2,1)}, bf16[2,64,896]{2,1,0:T(8,128)(2,1)S(1)}, u32[]{:S(2)}, u32[]{:S(2)}) collective-permute-start(bf16[2,64,896]{2,1,0:T(8,128)(2,1)} %get-tuple-element.62), channel_id=1, source_target_pairs={{0,6},{1,7},{2,4},{3,5},{4,2},{5,3},{6,0},{7,1},{8,14},{9,15},{10,... | collective-permute-start | bytes 688136 | tf_op jit(solution)/shard_map/ppermute | solution.py:17
  12.4 29.9 %collective-permute-start.13 = (bf16[2,64,896]{2,1,0:T(8,128)(2,1)}, bf16[2,64,896]{2,1,0:T(8,128)(2,1)S(1)}, u32[]{:S(2)}, u32[]{:S(2)}) collective-permute-start(bf16[2,64,896]{2,1,0:T(8,128)(2,1)} %get-tuple-element.63), channel_id=1, source_target_pairs={{0,5},{1,4},{2,7},{3,6},{4,1},{5,0},{6,3},{7,2},{8,13},{9,12},{10,... | collective-permute-start | bytes 688136 | tf_op jit(solution)/shard_map/ppermute | solution.py:17
  12.8 34.6 %collective-permute-start.14 = (bf16[2,64,896]{2,1,0:T(8,128)(2,1)}, bf16[2,64,896]{2,1,0:T(8,128)(2,1)S(1)}, u32[]{:S(2)}, u32[]{:S(2)}) collective-permute-start(bf16[2,64,896]{2,1,0:T(8,128)(2,1)} %get-tuple-element.64), channel_id=1, source_target_pairs={{0,4},{1,5},{2,6},{3,7},{4,0},{5,1},{6,2},{7,3},{8,12},{9,13},{10,... | collective-permute-start | bytes 688136 | tf_op jit(solution)/shard_map/ppermute | solution.py:17
  16.8 45.9 %collective-permute-start = (bf16[4,2,64,1152]{3,2,1,0:T(8,128)(2,1)S(1)}, bf16[4,2,64,1152]{3,2,1,0:T(8,128)(2,1)S(1)}, u32[]{:S(2)}, u32[]{:S(2)}) collective-permute-start(bf16[4,2,64,1152]{3,2,1,0:T(8,128)(2,1)S(1)} %lend_blocks.1), channel_id=1, source_target_pairs={{0,1},{1,0},{2,3},{3,2},{4,5},{5,4},{6,7},{7,6},{8,9},{9,8},{10,11... | collective-permute-start | bytes 3538952 | tf_op jit(solution)/shard_map/ppermute | solution.py:17
  24.3 25.4 %collective-permute-start.15 = (bf16[2,64,896]{2,1,0:T(8,128)(2,1)}, bf16[2,64,896]{2,1,0:T(8,128)(2,1)S(1)}, u32[]{:S(2)}, u32[]{:S(2)}) collective-permute-start(bf16[2,64,896]{2,1,0:T(8,128)(2,1)} %copy-done.7), channel_id=1, source_target_pairs={{0,3},{1,2},{2,1},{3,0},{4,7},{5,6},{6,5},{7,4},{8,11},{9,10},{10,... | collective-permute-start | bytes 688136 | tf_op jit(solution)/shard_map/ppermute | solution.py:17
  32.7 21.2 %collective-permute-start.16 = (bf16[2,64,896]{2,1,0:T(8,128)(2,1)}, bf16[2,64,896]{2,1,0:T(8,128)(2,1)}, u32[]{:S(2)}, u32[]{:S(2)}) collective-permute-start(bf16[2,64,896]{2,1,0:T(8,128)(2,1)} %copy-done.6), channel_id=1, source_target_pairs={{0,2},{1,3},{2,0},{3,1},{4,6},{5,7},{6,4},{7,5},{8,10},{9,11},{10,... | collective-permute-start | bytes 688136 | tf_op jit(solution)/shard_map/ppermute | solution.py:17
  42.3 11.6 %collective-permute-start.17 = (bf16[2,64,896]{2,1,0:T(8,128)(2,1)}, bf16[2,64,896]{2,1,0:T(8,128)(2,1)}, u32[]{:S(2)}, u32[]{:S(2)}) collective-permute-start(bf16[2,64,896]{2,1,0:T(8,128)(2,1)} %copy-done.5), channel_id=1, source_target_pairs={{0,1},{1,0},{2,3},{3,2},{4,5},{5,4},{6,7},{7,6},{8,9},{9,8},{10,11... | collective-permute-start | bytes 688136 | tf_op jit(solution)/shard_map/ppermute | solution.py:17
  48.1 16.3 %collective-permute-start.7 = (f32[2,4224]{1,0:T(2,128)}, f32[2,4224]{1,0:T(2,128)}, u32[]{:S(2)}, u32[]{:S(2)}) collective-permute-start(f32[2,4224]{1,0:T(2,128)} %get-tuple-element.159), channel_id=1, source_target_pairs={{0,16},{8,24},{16,0},{24,8},{1,17},{9,25},{17,1},{25,9},{2,18},{10... | collective-permute-start | bytes 101384 | tf_op jit(solution)/shard_map/ppermute | solution.py:17
  59.3 31.2 %collective-permute-start.18 = (bf16[2,128,896]{2,1,0:T(8,128)(2,1)}, bf16[2,128,896]{2,1,0:T(8,128)(2,1)S(1)}, u32[]{:S(2)}, u32[]{:S(2)}) collective-permute-start(bf16[2,128,896]{2,1,0:T(8,128)(2,1)} %get-tuple-element.78), channel_id=1, source_target_pairs={{0,8},{8,0},{16,24},{24,16},{1,9},{9,1},{17,25},{25,17},{2,10},{10... | collective-permute-start | bytes 1376264 | tf_op jit(solution)/shard_map/ppermute | solution.py:17
  60.8 32.7 %collective-permute-start.19 = (bf16[2,128,896]{2,1,0:T(8,128)(2,1)}, bf16[2,128,896]{2,1,0:T(8,128)(2,1)}, u32[]{:S(2)}, u32[]{:S(2)}) collective-permute-start(bf16[2,128,896]{2,1,0:T(8,128)(2,1)} %get-tuple-element.79), channel_id=1, source_target_pairs={{0,16},{8,24},{16,0},{24,8},{1,17},{9,25},{17,1},{25,9},{2,18},{10... | collective-permute-start | bytes 1376264 | tf_op jit(solution)/shard_map/ppermute | solution.py:17
  62.3 32.6 %collective-permute-start.20 = (bf16[2,128,896]{2,1,0:T(8,128)(2,1)}, bf16[2,128,896]{2,1,0:T(8,128)(2,1)}, u32[]{:S(2)}, u32[]{:S(2)}) collective-permute-start(bf16[2,128,896]{2,1,0:T(8,128)(2,1)} %get-tuple-element.80), channel_id=1, source_target_pairs={{0,24},{8,16},{16,8},{24,0},{1,25},{9,17},{17,9},{25,1},{2,26},{10... | collective-permute-start | bytes 1376264 | tf_op jit(solution)/shard_map/ppermute | solution.py:17
  66.0 22.5 %collective-permute-start.26 = (bf16[2,2,64,384]{3,2,1,0:T(8,128)(2,1)S(1)}, bf16[2,2,64,384]{3,2,1,0:T(8,128)(2,1)S(1)}, u32[]{:S(2)}, u32[]{:S(2)}) collective-permute-start(bf16[2,2,64,384]{3,2,1,0:T(8,128)(2,1)S(1)} %get-tuple-element.69), channel_id=1, source_target_pairs={{0,2},{1,3},{2,0},{3,1},{4,6},{5,7},{6,4},{7,5},{8,10},{9,11},{10,... | collective-permute-start | bytes 589832 | tf_op jit(solution)/shard_map/ppermute | solution.py:17
  66.4 10.3 %collective-permute-start.24 = (bf16[2,2,64,384]{3,2,1,0:T(8,128)(2,1)S(1)}, bf16[2,2,64,384]{3,2,1,0:T(8,128)(2,1)S(1)}, u32[]{:S(2)}, u32[]{:S(2)}) collective-permute-start(bf16[2,2,64,384]{3,2,1,0:T(8,128)(2,1)S(1)} %get-tuple-element.85), channel_id=1, source_target_pairs={{0,6},{1,7},{2,4},{3,5},{4,2},{5,3},{6,0},{7,1},{8,14},{9,15},{10,... | collective-permute-start | bytes 589832 | tf_op jit(solution)/shard_map/ppermute | solution.py:17
  88.5 25.0 %collective-permute-start.9 = (bf16[2,2,64,384]{3,2,1,0:T(8,128)(2,1)S(1)}, bf16[2,2,64,384]{3,2,1,0:T(8,128)(2,1)S(1)}, u32[]{:S(2)}, u32[]{:S(2)}) collective-permute-start(bf16[2,2,64,384]{3,2,1,0:T(8,128)(2,1)S(1)} %get-tuple-element.75), channel_id=1, source_target_pairs={{0,4},{1,5},{2,6},{3,7},{4,0},{5,1},{6,2},{7,3},{8,12},{9,13},{10,... | collective-permute-start | bytes 589832 | tf_op jit(solution)/shard_map/ppermute | solution.py:17
  90.4 30.9 %collective-permute-start.10 = (bf16[2,2,64,384]{3,2,1,0:T(8,128)(2,1)S(1)}, bf16[2,2,64,384]{3,2,1,0:T(8,128)(2,1)S(1)}, u32[]{:S(2)}, u32[]{:S(2)}) collective-permute-start(bf16[2,2,64,384]{3,2,1,0:T(8,128)(2,1)S(1)} %get-tuple-element.76), channel_id=1, source_target_pairs={{0,2},{1,3},{2,0},{3,1},{4,6},{5,7},{6,4},{7,5},{8,10},{9,11},{10,... | collective-permute-start | bytes 589832 | tf_op jit(solution)/shard_map/ppermute | solution.py:17
  93.5 31.4 %collective-permute-start.1 = (bf16[2,2,64,384]{3,2,1,0:T(8,128)(2,1)S(1)}, bf16[2,2,64,384]{3,2,1,0:T(8,128)(2,1)S(1)}, u32[]{:S(2)}, u32[]{:S(2)}) collective-permute-start(bf16[2,2,64,384]{3,2,1,0:T(8,128)(2,1)S(1)} %get-tuple-element.54), channel_id=1, source_target_pairs={{0,6},{1,7},{2,4},{3,5},{4,2},{5,3},{6,0},{7,1},{8,14},{9,15},{10,... | collective-permute-start | bytes 589832 | tf_op jit(solution)/shard_map/ppermute | solution.py:17
  94.9 30.5 %collective-permute-start.2 = (bf16[2,2,64,384]{3,2,1,0:T(8,128)(2,1)S(1)}, bf16[2,2,64,384]{3,2,1,0:T(8,128)(2,1)S(1)}, u32[]{:S(2)}, u32[]{:S(2)}) collective-permute-start(bf16[2,2,64,384]{3,2,1,0:T(8,128)(2,1)S(1)} %get-tuple-element.55), channel_id=1, source_target_pairs={{0,4},{1,5},{2,6},{3,7},{4,0},{5,1},{6,2},{7,3},{8,12},{9,13},{10,... | collective-permute-start | bytes 589832 | tf_op jit(solution)/shard_map/ppermute | solution.py:17
  96.7 30.2 %collective-permute-start.3 = (bf16[2,2,64,384]{3,2,1,0:T(8,128)(2,1)S(1)}, bf16[2,2,64,384]{3,2,1,0:T(8,128)(2,1)S(1)}, u32[]{:S(2)}, u32[]{:S(2)}) collective-permute-start(bf16[2,2,64,384]{3,2,1,0:T(8,128)(2,1)S(1)} %get-tuple-element.56), channel_id=1, source_target_pairs={{0,2},{1,3},{2,0},{3,1},{4,6},{5,7},{6,4},{7,5},{8,10},{9,11},{10,... | collective-permute-start | bytes 589832 | tf_op jit(solution)/shard_map/ppermute | solution.py:17
  113.5 15.0 %collective-permute-start.27 = (bf16[2,128,384]{2,1,0:T(8,128)(2,1)S(1)}, bf16[2,128,384]{2,1,0:T(8,128)(2,1)S(1)}, u32[]{:S(2)}, u32[]{:S(2)}) collective-permute-start(bf16[2,128,384]{2,1,0:T(8,128)(2,1)S(1)} %get-tuple-element.88), channel_id=1, source_target_pairs={{0,8},{8,0},{16,24},{24,16},{1,9},{9,1},{17,25},{25,17},{2,10},{10... | collective-permute-start | bytes 589832 | tf_op jit(solution)/shard_map/ppermute | solution.py:17
  121.4 14.1 %collective-permute-start.28 = (bf16[2,128,384]{2,1,0:T(8,128)(2,1)S(1)}, bf16[2,128,384]{2,1,0:T(8,128)(2,1)S(1)}, u32[]{:S(2)}, u32[]{:S(2)}) collective-permute-start(bf16[2,128,384]{2,1,0:T(8,128)(2,1)S(1)} %get-tuple-element.89), channel_id=1, source_target_pairs={{0,16},{8,24},{16,0},{24,8},{1,17},{9,25},{17,1},{25,9},{2,18},{10... | collective-permute-start | bytes 589832 | tf_op jit(solution)/shard_map/ppermute | solution.py:17
  124.9 10.7 %collective-permute-start.29 = (bf16[2,128,384]{2,1,0:T(8,128)(2,1)S(1)}, bf16[2,128,384]{2,1,0:T(8,128)(2,1)S(1)}, u32[]{:S(2)}, u32[]{:S(2)}) collective-permute-start(bf16[2,128,384]{2,1,0:T(8,128)(2,1)S(1)} %get-tuple-element.90), channel_id=1, source_target_pairs={{0,24},{8,16},{16,8},{24,0},{1,25},{9,17},{17,9},{25,1},{2,26},{10... | collective-permute-start | bytes 589832 | tf_op jit(solution)/shard_map/ppermute | solution.py:17
  125.4 12.2 %collective-permute-start.21 = (bf16[2,128,384]{2,1,0:T(8,128)(2,1)S(1)}, bf16[2,128,384]{2,1,0:T(8,128)(2,1)S(1)}, u32[]{:S(2)}, u32[]{:S(2)}) collective-permute-start(bf16[2,128,384]{2,1,0:T(8,128)(2,1)S(1)} %get-tuple-element.82), channel_id=1, source_target_pairs={{0,8},{8,0},{16,24},{24,16},{1,9},{9,1},{17,25},{25,17},{2,10},{10... | collective-permute-start | bytes 589832 | tf_op jit(solution)/shard_map/ppermute | solution.py:17
  126.9 15.9 %collective-permute-start.22 = (bf16[2,128,384]{2,1,0:T(8,128)(2,1)S(1)}, bf16[2,128,384]{2,1,0:T(8,128)(2,1)S(1)}, u32[]{:S(2)}, u32[]{:S(2)}) collective-permute-start(bf16[2,128,384]{2,1,0:T(8,128)(2,1)S(1)} %get-tuple-element.83), channel_id=1, source_target_pairs={{0,16},{8,24},{16,0},{24,8},{1,17},{9,25},{17,1},{25,9},{2,18},{10... | collective-permute-start | bytes 589832 | tf_op jit(solution)/shard_map/ppermute | solution.py:17
  128.4 14.4 %collective-permute-start.23 = (bf16[2,128,384]{2,1,0:T(8,128)(2,1)S(1)}, bf16[2,128,384]{2,1,0:T(8,128)(2,1)S(1)}, u32[]{:S(2)}, u32[]{:S(2)}) collective-permute-start(bf16[2,128,384]{2,1,0:T(8,128)(2,1)S(1)} %get-tuple-element.84), channel_id=1, source_target_pairs={{0,24},{8,16},{16,8},{24,0},{1,25},{9,17},{17,9},{25,1},{2,26},{10... | collective-permute-start | bytes 589832 | tf_op jit(solution)/shard_map/ppermute | solution.py:17
  135.5 10.9 %collective-permute-start.4 = (bf16[2,128,384]{2,1,0:T(8,128)(2,1)S(1)}, bf16[2,128,384]{2,1,0:T(8,128)(2,1)S(1)}, u32[]{:S(2)}, u32[]{:S(2)}) collective-permute-start(bf16[2,128,384]{2,1,0:T(8,128)(2,1)S(1)} %get-tuple-element.58), channel_id=1, source_target_pairs={{0,8},{8,0},{16,24},{24,16},{1,9},{9,1},{17,25},{25,17},{2,10},{10... | collective-permute-start | bytes 589832 | tf_op jit(solution)/shard_map/ppermute | solution.py:17
  135.5 10.9 %collective-permute-start.5 = (bf16[2,128,384]{2,1,0:T(8,128)(2,1)S(1)}, bf16[2,128,384]{2,1,0:T(8,128)(2,1)S(1)}, u32[]{:S(2)}, u32[]{:S(2)}) collective-permute-start(bf16[2,128,384]{2,1,0:T(8,128)(2,1)S(1)} %get-tuple-element.59), channel_id=1, source_target_pairs={{0,16},{8,24},{16,0},{24,8},{1,17},{9,25},{17,1},{25,9},{2,18},{10... | collective-permute-start | bytes 589832 | tf_op jit(solution)/shard_map/ppermute | solution.py:17
  159.1 11.3 %collective-permute-start.40 = (bf16[4,2,256,128]{3,2,1,0:T(8,128)(2,1)S(1)}, bf16[4,2,256,128]{3,2,1,0:T(8,128)(2,1)S(1)}, u32[]{:S(2)}, u32[]{:S(2)}) collective-permute-start(bf16[4,2,256,128]{3,2,1,0:T(8,128)(2,1)S(1)} %get-tuple-element.102), channel_id=1, source_target_pairs={{0,1},{1,0},{2,3},{3,2},{4,5},{5,4},{6,7},{7,6},{8,9},{9,8},{10,11... | collective-permute-start | bytes 1572872 | tf_op jit(solution)/shard_map/ppermute | solution.py:17
  173.1 15.0 %collective-permute-start.42 = (bf16[2,256,128]{2,1,0:T(8,128)(2,1)S(1)}, bf16[2,256,128]{2,1,0:T(8,128)(2,1)S(1)}, u32[]{:S(2)}, u32[]{:S(2)}) collective-permute-start(bf16[2,256,128]{2,1,0:T(8,128)(2,1)S(1)} %get-tuple-element.114), channel_id=1, source_target_pairs={{0,4},{1,5},{2,6},{3,7},{4,0},{5,1},{6,2},{7,3},{8,12},{9,13},{10,... | collective-permute-start | bytes 393224 | tf_op jit(solution)/shard_map/ppermute | solution.py:17
  175.0 13.2 %collective-permute-start.34 = (bf16[2,256,128]{2,1,0:T(8,128)(2,1)S(1)}, bf16[2,256,128]{2,1,0:T(8,128)(2,1)S(1)}, u32[]{:S(2)}, u32[]{:S(2)}) collective-permute-start(bf16[2,256,128]{2,1,0:T(8,128)(2,1)S(1)} %get-tuple-element.109), channel_id=1, source_target_pairs={{0,6},{1,7},{2,4},{3,5},{4,2},{5,3},{6,0},{7,1},{8,14},{9,15},{10,... | collective-permute-start | bytes 393224 | tf_op jit(solution)/shard_map/ppermute | solution.py:17
  177.7 11.9 %collective-permute-start.36 = (bf16[2,256,128]{2,1,0:T(8,128)(2,1)S(1)}, bf16[2,256,128]{2,1,0:T(8,128)(2,1)S(1)}, u32[]{:S(2)}, u32[]{:S(2)}) collective-permute-start(bf16[2,256,128]{2,1,0:T(8,128)(2,1)S(1)} %get-tuple-element.110), channel_id=1, source_target_pairs={{0,2},{1,3},{2,0},{3,1},{4,6},{5,7},{6,4},{7,5},{8,10},{9,11},{10,... | collective-permute-start | bytes 393224 | tf_op jit(solution)/shard_map/ppermute | solution.py:17
  178.7 17.3 %collective-permute-start.35 = (bf16[2,256,128]{2,1,0:T(8,128)(2,1)S(1)}, bf16[2,256,128]{2,1,0:T(8,128)(2,1)S(1)}, u32[]{:S(2)}, u32[]{:S(2)}) collective-permute-start(bf16[2,256,128]{2,1,0:T(8,128)(2,1)S(1)} %get-tuple-element.111), channel_id=1, source_target_pairs={{0,4},{1,5},{2,6},{3,7},{4,0},{5,1},{6,2},{7,3},{8,12},{9,13},{10,... | collective-permute-start | bytes 393224 | tf_op jit(solution)/shard_map/ppermute | solution.py:17
  (24 other events, 121.9 us)
where the time goes:
time: 198 us; the launch traced here: 197 us
  starting transfers between devices  70.1 us (35%)
  waiting for transfers between devices  66.8 us (34%)
  Pallas kernels  40.7 us (21%)
  local copies, waits for them, and re-layouts  11.7 us (6%)
  other arithmetic  7.11 us (4%)
    ppermute x44, starting transfers between devices, swap(): return lax.ppermute(block, axis, [(i, i ^ mask) for i in range(count)])  70.1 us
    ppermute x44, waiting for transfers between devices, swap(): return lax.ppermute(block, axis, [(i, i ^ mask) for i in range(count)])  66.8 us
    pallas_call x4, Pallas kernels, merge_blocks(): pl.pallas_call(functools.partial(merge_kernel, levels, subs, given, final...  16.7 us
    pallas_call x4, Pallas kernels, steer_blocks(): pl.pallas_call(functools.partial(steer_kernel, count, subs, None if lent...  9.08 us
    unnamed x25, local copies, waits for them, and re-layouts  5.33 us
    pallas_call x2, Pallas kernels, cut_blocks(): pl.pallas_call(functools.partial(cut_kernel, chosen, first), out_shape=[j...  5.03 us
    pallas_call x3, Pallas kernels, join_blocks(): pl.pallas_call(functools.partial(join_kernel, chosen, first, first - behi...  4.7 us
  transfers between devices with their start and end apart: 44, of which 18 were waited for; matrix products, arithmetic and copies ran while one was open for 6% of the time, Pallas kernels for 17%

commit v1 on v0

--- a/solution.py
+++ b/solution.py
@@ -32,23 +32,8 @@
     return list(range(count - 1, 0, -1))
 
 
-def lanes(start):
-    return pl.multiple_of(start, 128)
-
-
-def window(shape, offsets):
-    return pl.BlockSpec(tuple(pl.Element(size) for size in shape), offsets)
-
-
 def params():
     return pltpu.CompilerParams(vmem_limit_bytes=GRANT)
-
-
-def block_of(rows, unit, first, pick):
-    def offsets(i, ids_ref):
-        return 0, pl.multiple_of(ids_ref[pick] * rows, rows), lanes(first + i * unit)
-
-    return window((2, rows, unit), offsets)
 
 
 def resident():
@@ -128,6 +113,9 @@
     ]
     for copy in copies:
         copy.start()
+    own = fetch(echoes_ref, ids_ref, 0, first, outs[-1], sems.at[len(chosen)])
+    own.start()
+    copies.append(own)
     for place, d in enumerate(chosen):
         outs[place][1] = lent_ref[d, :, :, start : start + outs[place].shape[3]]
     for copy in copies:
@@ -138,13 +126,14 @@
     chosen = masks(lax.axis_size("tile") // 2)
     return pl.pallas_call(
         functools.partial(join_kernel, chosen, first, first - behind),
-        out_shape=[jax.ShapeDtypeStruct((2, 2, rows, unit), echoes.dtype)] * len(chosen),
+        out_shape=[jax.ShapeDtypeStruct((2, 2, rows, unit), echoes.dtype)] * len(chosen)
+        + [jax.ShapeDtypeStruct((2, rows, unit), echoes.dtype)],
         grid_spec=pltpu.PrefetchScalarGridSpec(
             num_scalar_prefetch=1,
             grid=(1,),
             in_specs=[pl.BlockSpec(memory_space=pl.ANY), resident()],
-            out_specs=[resident()] * len(chosen),
-            scratch_shapes=[pltpu.SemaphoreType.DMA((len(chosen),))],
+            out_specs=[resident()] * (len(chosen) + 1),
+            scratch_shapes=[pltpu.SemaphoreType.DMA((len(chosen) + 1,))],
         ),
         compiler_params=params(),
         cost_estimate=cost(0, 16 * len(chosen) * rows * unit),
@@ -172,28 +161,27 @@
         outs[r][...] = held[r]
 
 
-def steer_blocks(echoes, lent, arrived, weights, ids, first, behind, unit, rows, after):
+def steer_blocks(own, lent, arrived, weights, ids, first, behind, after):
     count, subs = lax.axis_size("tile"), lax.axis_size("sub")
     pieces = count // subs
-    height = weights.shape[0]
+    height, unit = weights.shape[0], own.shape[2]
     operands = ([] if lent is None else [lent]) + arrived
     shape = (pieces, height, unit)
     return pl.pallas_call(
         functools.partial(steer_kernel, count, subs, None if lent is None else first - behind),
-        out_shape=[jax.ShapeDtypeStruct(shape, echoes.dtype)] * subs,
+        out_shape=[jax.ShapeDtypeStruct(shape, own.dtype)] * subs,
         grid_spec=pltpu.PrefetchScalarGridSpec(
             num_scalar_prefetch=1,
             grid=(1,),
-            in_specs=[resident(), block_of(rows, unit, first, 0)]
-            + [resident()] * len(operands)
+            in_specs=[resident()] * (2 + len(operands))
             + [pl.BlockSpec(memory_space=pl.ANY)] * len(after),
             out_specs=[resident()] * subs,
-            scratch_shapes=[pltpu.VMEM((subs,) + shape, echoes.dtype)],
+            scratch_shapes=[pltpu.VMEM((subs,) + shape, own.dtype)],
         ),
         compiler_params=params(),
         cost_estimate=cost(2 * count * height * height * unit, 4 * count * height * unit),
         name="steer_blocks",
-    )(ids, weights, echoes, *operands, *after)
+    )(ids, weights, own, *operands, *after)
 
 
 def turned(block, cosine, sine):
@@ -321,37 +309,34 @@
 
 def beam_kernel(subs, foot, ids_ref, *refs):
     pieces = refs[:subs]
-    near_ref, far_ref, keep_ref, send_ref, held = refs[subs:]
-    step = pl.program_id(0)
-    count = pl.num_programs(0)
-
-    @pl.when(step == 0)
-    def _():
-        total = pieces[0][...].astype(jnp.float32)
-        for piece in pieces[1:]:
-            total = total + piece[...].astype(jnp.float32)
-        held[...] = total.astype(held.dtype)
-
-    planes = keep_ref.shape[1]
+    map_ref, keep_ref, send_ref, held = refs[subs:]
+    count, planes = keep_ref.shape[:2]
     depth = held.shape[0] // planes
-    for side, map_ref, out_ref in ((0, near_ref, keep_ref), (1, far_ref, send_ref)):
-        tile = ids_ref[2 * step + side]
-        covered = ids_ref[2 * count] == tile
-        for entry in range(1, foot):
-            covered = jnp.logical_or(covered, ids_ref[2 * count + entry] == tile)
-
-        @pl.when(covered)
-        def _():
-            for plane in range(planes):
-                out_ref[step, plane] = jnp.dot(
-                    map_ref[0],
-                    held[plane * depth : (plane + 1) * depth],
-                    preferred_element_type=jnp.float32,
-                ).astype(out_ref.dtype)
-
-        @pl.when(jnp.logical_not(covered))
-        def _():
-            out_ref[step] = jnp.zeros(out_ref.shape[1:], out_ref.dtype)
+    total = pieces[0][...].astype(jnp.float32)
+    for piece in pieces[1:]:
+        total = total + piece[...].astype(jnp.float32)
+    held[...] = total.astype(held.dtype)
+
+    @pl.loop(0, count)
+    def _(step):
+        for side, out_ref in ((1, send_ref), (0, keep_ref)):
+            tile = ids_ref[2 * step + side]
+            covered = ids_ref[2 * count] == tile
+            for entry in range(1, foot):
+                covered = jnp.logical_or(covered, ids_ref[2 * count + entry] == tile)
+
+            @pl.when(covered)
+            def _():
+                for plane in range(planes):
+                    out_ref[step, plane] = jnp.dot(
+                        map_ref[tile],
+                        held[plane * depth : (plane + 1) * depth],
+                        preferred_element_type=jnp.float32,
+                    ).astype(out_ref.dtype)
+
+            @pl.when(jnp.logical_not(covered))
+            def _():
+                out_ref[step] = jnp.zeros(out_ref.shape[1:], out_ref.dtype)
 
 
 def beam_blocks(pieces, beam_map, ids):
@@ -360,9 +345,6 @@
     height, width = pieces[0].shape
     planes = height // depth
     shape = (count, planes, rows, width)
-
-    def pick(side):
-        return pl.BlockSpec((1, rows, depth), lambda i, ids_ref: (ids_ref[2 * i + side], 0, 0))
 
     return pl.pallas_call(
         functools.partial(beam_kernel, len(pieces), ids.shape[0] - tiles),
@@ -372,16 +354,15 @@
         ],
         grid_spec=pltpu.PrefetchScalarGridSpec(
             num_scalar_prefetch=1,
-            grid=(count,),
-            in_specs=[resident()] * len(pieces)
-            + [pick(0), pick(1)],
+            grid=(1,),
+            in_specs=[resident()] * (len(pieces) + 1),
             out_specs=[resident(), resident()],
             scratch_shapes=[pltpu.VMEM((height, width), jnp.bfloat16)],
         ),
         compiler_params=params(),
         cost_estimate=cost(2 * tiles * rows * depth * planes * width, 2 * beam_map.size),
         name="beam_blocks",
-    )(ids, *pieces, beam_map, beam_map)
+    )(ids, *pieces, beam_map)
 
 
 def own_first(pair, upper):
@@ -465,8 +446,9 @@
     opening = stretches[0][1]
 
     cuts = []
-    for chosen in (masks(tiles)[:2], masks(tiles)[2:]):
+    for chosen in (masks(tiles)[:2], masks(tiles)[2:] + [0]):
         cuts += cut_blocks(echoes, ids, chosen, 0, opening, base)
+    owns = [cuts[-1]]
     arrived = [[swap(cut, "tile", k) for cut, k in zip(cuts, masks(tiles))]]
     lent = lend_blocks(echoes, ids, opening, local - opening, base)
     lent = swap(lent, "tile", 1)
@@ -481,6 +463,7 @@
     packets = angle_packets(angles[0, 0], local * tiles, base, local * pieces)
     for part_id, (first, length) in list(enumerate(stretches))[1:]:
         joined = join_blocks(echoes, lent, ids, first, opening, length, base)
+        owns.append(joined[-1])
         arrived.append([swap(part, "tile", 2 * d) for part, d in zip(joined, masks(tiles // 2))])
         if part_id == 1:
             interp, packets, _ = lax.optimization_barrier((interp, packets, joined[-1]))
@@ -490,17 +473,15 @@
     map_rows = pltpu.with_memory_space_constraint(map_rows, pltpu.HBM)
 
     totals = [None, None]
-    for (first, length), blocks in zip(stretches, arrived):
+    for part_id, ((first, length), blocks) in enumerate(zip(stretches, arrived)):
         parts = steer_blocks(
-            echoes,
+            owns[part_id],
             lent if first else None,
             blocks,
             steer,
             ids,
             first,
             opening,
-            length,
-            base,
             [] if totals[-2] is None or first + length == local else [totals[-2]],
         )
         parts = [parts[0]] + [swap(parts[r], "sub", r) for r in range(1, subs)]

time: 198 us -> 191 us (0.965)
  waiting for transfers between devices: 66.8 us -> 61.3 us
  starting transfers between devices: 70.1 us -> 73.7 us
  Pallas kernels: 40.7 us -> 37.5 us
    ppermute x44, waiting for transfers between devices: 66.8 us -> 61.3 us  [swap(): return lax.ppermute(block, axis, [(i, i ^ mask) for i in range(count)])]
    ppermute x44, starting transfers between devices: 70.1 us -> 73.7 us  [swap(): return lax.ppermute(block, axis, [(i, i ^ mask) for i in range(count)])]
    pallas_call x4, Pallas kernels: 9.08 us -> 6.37 us  [steer_blocks(): pl.pallas_call(functools.partial(steer_kernel, count, subs, None if lent...]
  transfers between devices with their start and end apart: 44 -> 44, of which waited for: 18 -> 18; matrix products, arithmetic and copies ran while one was open for 6% -> 6% of each run, Pallas kernels for 17% -> 16%
where the time goes in v1:
time: 191 us
  starting transfers between devices  73.7 us (39%)
  waiting for transfers between devices  61.3 us (32%)
  Pallas kernels  37.5 us (20%)
  local copies, waits for them, and re-layouts  10.9 us (6%)
  other arithmetic  6.51 us (3%)
    ppermute x44, starting transfers between devices, swap(): return lax.ppermute(block, axis, [(i, i ^ mask) for i in range(count)])  73.7 us
    ppermute x44, waiting for transfers between devices, swap(): return lax.ppermute(block, axis, [(i, i ^ mask) for i in range(count)])  61.3 us
    pallas_call x4, Pallas kernels, merge_blocks(): pl.pallas_call(functools.partial(merge_kernel, levels, subs, given, final...  16.7 us
    pallas_call x4, Pallas kernels, steer_blocks(): pl.pallas_call(functools.partial(steer_kernel, count, subs, None if lent...  6.37 us
    unnamed x25, local copies, waits for them, and re-layouts  5.3 us
    pallas_call x3, Pallas kernels, join_blocks(): pl.pallas_call(functools.partial(join_kernel, chosen, first, first - behi...  4.87 us
    pallas_call x2, Pallas kernels, cut_blocks(): pl.pallas_call(functools.partial(cut_kernel, chosen, first), out_shape=[j...  4.55 us
  transfers between devices with their start and end apart: 44, of which 18 were waited for; matrix products, arithmetic and copies ran while one was open for 6% of the time, Pallas kernels for 16%

profile of v1, /device:TPU:0, one launch (start us, length us, event | category | flops | bytes accessed | tf_op | source)
XLA Modules:
  0.0 190.5 jit_solution(7676381052546550394)
XLA Ops:
  0.1 2.9 %cut_blocks.3 = (bf16[2,64,896]{2,1,0:T(8,128)(2,1)}, bf16[2,64,896]{2,1,0:T(8,128)(2,1)}, bf16[2,64,896]{2,1,0:T(8,128)(2,1)}, bf16[2,64,896]{2,1,0:T(8,128)(2,...) custom-call(s32[24]{0:T(128)S(1)} %stack.158.ids_ref, bf16[2,512,2048]{2,1,0:T(8,128)(2,1)} %echoes_ref.11), custom_call_target="tpu_custom_call" | custom-call | bytes 2752512 | tf_op jit(solution)/shard_map/cut_blocks/pallas_call | solution.py:63
  3.7 3.5 %collective-permute-start.13 = (bf16[2,64,896]{2,1,0:T(8,128)(2,1)}, bf16[2,64,896]{2,1,0:T(8,128)(2,1)S(1)}, u32[]{:S(2)}, u32[]{:S(2)}) collective-permute-start(bf16[2,64,896]{2,1,0:T(8,128)(2,1)} %get-tuple-element.68), channel_id=1, source_target_pairs={{0,5},{1,4},{2,7},{3,6},{4,1},{5,0},{6,3},{7,2},{8,13},{9,12},{10,... | collective-permute-start | bytes 688136 | tf_op jit(solution)/shard_map/ppermute | solution.py:17
  9.5 1.8 lend_blocks.1
  21.0 1.7 collective-permute-done.13.refs_2_
  24.2 4.2 %collective-permute-done.14.refs_3_ = bf16[2,64,896]{2,1,0:T(8,128)(2,1)S(1)} collective-permute-done((bf16[2,64,896]{2,1,0:T(8,128)(2,1)}, bf16[2,64,896]{2,1,0:T(8,128)(2,1)S(1)}, u32[]{:S(2)}, u32[]{:S(2)}) %collective-permute-start.14) | collective-permute-done | bytes 229408 | tf_op jit(solution)/shard_map/ppermute | solution.py:17
  28.5 3.8 %collective-permute-start.11 = (bf16[2,64,896]{2,1,0:T(8,128)(2,1)}, bf16[2,64,896]{2,1,0:T(8,128)(2,1)}, u32[]{:S(2)}, u32[]{:S(2)}) collective-permute-start(bf16[2,64,896]{2,1,0:T(8,128)(2,1)} %copy-done.7), channel_id=1, source_target_pairs={{0,7},{1,6},{2,5},{3,4},{4,3},{5,2},{6,1},{7,0},{8,15},{9,14},{10,... | collective-permute-start | bytes 688136 | tf_op jit(solution)/shard_map/ppermute | solution.py:17
  38.6 5.1 %collective-permute-done.12.refs_1_ = bf16[2,64,896]{2,1,0:T(8,128)(2,1)} collective-permute-done((bf16[2,64,896]{2,1,0:T(8,128)(2,1)}, bf16[2,64,896]{2,1,0:T(8,128)(2,1)}, u32[]{:S(2)}, u32[]{:S(2)}) %collective-permute-start.12) | collective-permute-done | bytes 229408 | tf_op jit(solution)/shard_map/ppermute | solution.py:17
  45.6 3.5 %steer_blocks.5 = (bf16[2,128,896]{2,1,0:T(8,128)(2,1)S(1)}, bf16[2,128,896]{2,1,0:T(8,128)(2,1)}, bf16[2,128,896]{2,1,0:T(8,128)(2,1)}, bf16[2,128,896]{2,1,0:T(8,128)(2,1)}) custom-call(s32[24]{0:T(128)S(1)} %stack.158.ids_ref, bf16[128,128]{1,0:T(8,128)(2,1)S(1)} %maximum_maximum_fusion.2.weights_ref, bf16[2,64,896]{2,1,0:T(8,128)(2,1)S(1)} %get-tuple-element.73.own_ref, ...), custom_call_target="tpu_custom_call" | custom-call | flops 234881024 | bytes 3670016 | tf_op jit(solution)/shard_map/steer_blocks/pallas_call | solution.py:170
  49.1 1.9 collective-permute-start.18
  56.6 3.9 %collective-permute-start.24 = (bf16[2,2,64,384]{3,2,1,0:T(8,128)(2,1)S(1)}, bf16[2,2,64,384]{3,2,1,0:T(8,128)(2,1)S(1)}, u32[]{:S(2)}, u32[]{:S(2)}) collective-permute-start(bf16[2,2,64,384]{3,2,1,0:T(8,128)(2,1)S(1)} %get-tuple-element.92), channel_id=1, source_target_pairs={{0,6},{1,7},{2,4},{3,5},{4,2},{5,3},{6,0},{7,1},{8,14},{9,15},{10,... | collective-permute-start | bytes 589832 | tf_op jit(solution)/shard_map/ppermute | solution.py:17
  60.5 6.6 %collective-permute-start.25 = (bf16[2,2,64,384]{3,2,1,0:T(8,128)(2,1)S(1)}, bf16[2,2,64,384]{3,2,1,0:T(8,128)(2,1)S(1)}, u32[]{:S(2)}, u32[]{:S(2)}) collective-permute-start(bf16[2,2,64,384]{3,2,1,0:T(8,128)(2,1)S(1)} %get-tuple-element.93), channel_id=1, source_target_pairs={{0,4},{1,5},{2,6},{3,7},{4,0},{5,1},{6,2},{7,3},{8,12},{9,13},{10,... | collective-permute-start | bytes 589832 | tf_op jit(solution)/shard_map/ppermute | solution.py:17
  70.7 6.1 %collective-permute-start.26 = (bf16[2,2,64,384]{3,2,1,0:T(8,128)(2,1)S(1)}, bf16[2,2,64,384]{3,2,1,0:T(8,128)(2,1)S(1)}, u32[]{:S(2)}, u32[]{:S(2)}) collective-permute-start(bf16[2,2,64,384]{3,2,1,0:T(8,128)(2,1)S(1)} %get-tuple-element.94), channel_id=1, source_target_pairs={{0,2},{1,3},{2,0},{3,1},{4,6},{5,7},{6,4},{7,5},{8,10},{9,11},{10,... | collective-permute-start | bytes 589832 | tf_op jit(solution)/shard_map/ppermute | solution.py:17
  77.0 2.5 %collective-permute-done.25.refs_2_ = bf16[2,2,64,384]{3,2,1,0:T(8,128)(2,1)S(1)} collective-permute-done((bf16[2,2,64,384]{3,2,1,0:T(8,128)(2,1)S(1)}, bf16[2,2,64,384]{3,2,1,0:T(8,128)(2,1)S(1)}, u32[]{:S(2)}, u32[]{:S(2)}) %collective-permute-start.25) | collective-permute-done | bytes 196640 | tf_op jit(solution)/shard_map/ppermute | solution.py:17
  79.5 4.2 %collective-permute-done.26.refs_3_ = bf16[2,2,64,384]{3,2,1,0:T(8,128)(2,1)S(1)} collective-permute-done((bf16[2,2,64,384]{3,2,1,0:T(8,128)(2,1)S(1)}, bf16[2,2,64,384]{3,2,1,0:T(8,128)(2,1)S(1)}, u32[]{:S(2)}, u32[]{:S(2)}) %collective-permute-start.26) | collective-permute-done | bytes 196640 | tf_op jit(solution)/shard_map/ppermute | solution.py:17
  86.2 2.6 %collective-permute-start.1 = (bf16[2,2,64,384]{3,2,1,0:T(8,128)(2,1)S(1)}, bf16[2,2,64,384]{3,2,1,0:T(8,128)(2,1)S(1)}, u32[]{:S(2)}, u32[]{:S(2)}) collective-permute-start(bf16[2,2,64,384]{3,2,1,0:T(8,128)(2,1)S(1)} %get-tuple-element.59), channel_id=1, source_target_pairs={{0,6},{1,7},{2,4},{3,5},{4,2},{5,3},{6,0},{7,1},{8,14},{9,15},{10,... | collective-permute-start | bytes 589832 | tf_op jit(solution)/shard_map/ppermute | solution.py:17
  88.8 1.8 collective-permute-start.2
  90.7 2.6 %collective-permute-done.8.refs_1_ = bf16[2,2,64,384]{3,2,1,0:T(8,128)(2,1)S(1)} collective-permute-done((bf16[2,2,64,384]{3,2,1,0:T(8,128)(2,1)S(1)}, bf16[2,2,64,384]{3,2,1,0:T(8,128)(2,1)S(1)}, u32[]{:S(2)}, u32[]{:S(2)}) %collective-permute-start.8) | collective-permute-done | bytes 196640 | tf_op jit(solution)/shard_map/ppermute | solution.py:17
  94.8 6.4 %merge_blocks.4.refs_4_.refs_8_ = f32[512,1024]{1,0:T(8,128)S(1)} custom-call(s32[4]{0:T(128)S(1)} %pad_add_fusion.ids_ref, bf16[2,128,896]{2,1,0:T(8,128)(2,1)S(1)} %get-tuple-element.84.refs_0_, bf16[2,128,896]{2,1,0:T(8,128)(2,1)S(1)} %collective-permute-done.18.refs_1_, bf16[2,128,896]{2,1,0:T(8,128)(2,1)} %collective-permute-done.19.refs_2_, ...), custom_call_target="tpu_custom_call" | custom-call | flops 3288334336 | bytes 5505024 | tf_op jit(solution)/shard_map/merge_blocks/pallas_call | solution.py:290
  101.2 10.1 %collective-permute-done.9.refs_2_ = bf16[2,2,64,384]{3,2,1,0:T(8,128)(2,1)S(1)} collective-permute-done((bf16[2,2,64,384]{3,2,1,0:T(8,128)(2,1)S(1)}, bf16[2,2,64,384]{3,2,1,0:T(8,128)(2,1)S(1)}, u32[]{:S(2)}, u32[]{:S(2)}) %collective-permute-start.9) | collective-permute-done | bytes 196640 | tf_op jit(solution)/shard_map/ppermute | solution.py:17
  115.2 3.1 %collective-permute-done.2.refs_2_ = bf16[2,2,64,384]{3,2,1,0:T(8,128)(2,1)S(1)} collective-permute-done((bf16[2,2,64,384]{3,2,1,0:T(8,128)(2,1)S(1)}, bf16[2,2,64,384]{3,2,1,0:T(8,128)(2,1)S(1)}, u32[]{:S(2)}, u32[]{:S(2)}) %collective-permute-start.2) | collective-permute-done | bytes 196640 | tf_op jit(solution)/shard_map/ppermute | solution.py:17
  125.9 2.6 %collective-permute-start.6 = (bf16[2,128,384]{2,1,0:T(8,128)(2,1)S(1)}, bf16[2,128,384]{2,1,0:T(8,128)(2,1)S(1)}, u32[]{:S(2)}, u32[]{:S(2)}) collective-permute-start(bf16[2,128,384]{2,1,0:T(8,128)(2,1)S(1)} %get-tuple-element.65), channel_id=1, source_target_pairs={{0,24},{8,16},{16,8},{24,0},{1,25},{9,17},{17,9},{25,1},{2,26},{10... | collective-permute-start | bytes 589832 | tf_op jit(solution)/shard_map/ppermute | solution.py:17
  128.6 3.7 %merge_blocks.5.refs_8_ = f32[512,1024]{1,0:T(8,128)S(1)} custom-call(s32[4]{0:T(128)S(1)} %pad_add_fusion.ids_ref, bf16[2,128,384]{2,1,0:T(8,128)(2,1)S(1)} %get-tuple-element.95.refs_0_, bf16[2,128,384]{2,1,0:T(8,128)(2,1)S(1)} %collective-permute-done.27.refs_1_, ...), custom_call_target="tpu_custom_call", output_to_operand_aliasing={{}: (9, {})} | custom-call | flops 1409286144 | bytes 2359296 | tf_op jit(solution)/shard_map/merge_blocks/pallas_call | solution.py:290
  132.4 3.6 %merge_blocks.6.refs_8_ = f32[512,1024]{1,0:T(8,128)S(1)} custom-call(s32[4]{0:T(128)S(1)} %pad_add_fusion.ids_ref, bf16[2,128,384]{2,1,0:T(8,128)(2,1)S(1)} %get-tuple-element.88.refs_0_, bf16[2,128,384]{2,1,0:T(8,128)(2,1)S(1)} %collective-permute-done.21.refs_1_, ...), custom_call_target="tpu_custom_call", output_to_operand_aliasing={{}: (9, {})} | custom-call | flops 1409286144 | bytes 2359296 | tf_op jit(solution)/shard_map/merge_blocks/pallas_call | solution.py:290
  135.9 2.1 %collective-permute-done.5.refs_2_ = bf16[2,128,384]{2,1,0:T(8,128)(2,1)S(1)} collective-permute-done((bf16[2,128,384]{2,1,0:T(8,128)(2,1)S(1)}, bf16[2,128,384]{2,1,0:T(8,128)(2,1)S(1)}, u32[]{:S(2)}, u32[]{:S(2)}) %collective-permute-start.5) | collective-permute-done | bytes 196640 | tf_op jit(solution)/shard_map/ppermute | solution.py:17
  138.0 2.9 %merge_blocks.7 = (bf16[512,128]{1,0:T(8,128)(2,1)S(1)}, bf16[512,128]{1,0:T(8,128)(2,1)S(1)}, bf16[512,128]{1,0:T(8,128)(2,1)S(1)}, bf16[512,128]{1,0:T(8,128)(...) custom-call(s32[4]{0:T(128)S(1)} %pad_add_fusion.ids_ref, ...), custom_call_target="tpu_custom_call" | custom-call | flops 1409286144 | bytes 2359296 | tf_op jit(solution)/shard_map/merge_blocks/pallas_call | solution.py:290
  154.0 2.8 %collective-permute-done.37.refs_1_ = bf16[512,128]{1,0:T(8,128)(2,1)S(1)} collective-permute-done((bf16[512,128]{1,0:T(8,128)(2,1)S(1)}, bf16[512,128]{1,0:T(8,128)(2,1)S(1)}, u32[]{:S(2)}, u32[]{:S(2)}) %collective-permute-start.37) | collective-permute-done | bytes 131104 | tf_op jit(solution)/shard_map/ppermute | solution.py:17
  156.8 3.6 %collective-permute-done.38.refs_2_ = bf16[512,128]{1,0:T(8,128)(2,1)S(1)} collective-permute-done((bf16[512,128]{1,0:T(8,128)(2,1)S(1)}, bf16[512,128]{1,0:T(8,128)(2,1)S(1)}, u32[]{:S(2)}, u32[]{:S(2)}) %collective-permute-start.38) | collective-permute-done | bytes 131104 | tf_op jit(solution)/shard_map/ppermute | solution.py:17
  163.8 2.3 %collective-permute-start.35 = (bf16[2,256,128]{2,1,0:T(8,128)(2,1)S(1)}, bf16[2,256,128]{2,1,0:T(8,128)(2,1)S(1)}, u32[]{:S(2)}, u32[]{:S(2)}) collective-permute-start(bf16[2,256,128]{2,1,0:T(8,128)(2,1)S(1)} %get-tuple-element.119), channel_id=1, source_target_pairs={{0,4},{1,5},{2,6},{3,7},{4,0},{5,1},{6,2},{7,3},{8,12},{9,13},{10,... | collective-permute-start | bytes 393224 | tf_op jit(solution)/shard_map/ppermute | solution.py:17
  166.8 1.9 %collective-permute-start.41 = (bf16[2,256,128]{2,1,0:T(8,128)(2,1)S(1)}, bf16[2,256,128]{2,1,0:T(8,128)(2,1)S(1)}, u32[]{:S(2)}, u32[]{:S(2)}) collective-permute-start(bf16[2,256,128]{2,1,0:T(8,128)(2,1)S(1)} %get-tuple-element.120), channel_id=1, source_target_pairs={{0,6},{1,7},{2,4},{3,5},{4,2},{5,3},{6,0},{7,1},{8,14},{9,15},{10,... | collective-permute-start | bytes 393224 | tf_op jit(solution)/shard_map/ppermute | solution.py:17
  170.5 6.1 %collective-permute-start.43 = (bf16[2,256,128]{2,1,0:T(8,128)(2,1)S(1)}, bf16[2,256,128]{2,1,0:T(8,128)(2,1)S(1)}, u32[]{:S(2)}, u32[]{:S(2)}) collective-permute-start(bf16[2,256,128]{2,1,0:T(8,128)(2,1)S(1)} %get-tuple-element.121), channel_id=1, source_target_pairs={{0,2},{1,3},{2,0},{3,1},{4,6},{5,7},{6,4},{7,5},{8,10},{9,11},{10,... | collective-permute-start | bytes 393224 | tf_op jit(solution)/shard_map/ppermute | solution.py:17
  176.7 7.4 %collective-permute-done.35 = bf16[2,256,128]{2,1,0:T(8,128)(2,1)S(1)} collective-permute-done((bf16[2,256,128]{2,1,0:T(8,128)(2,1)S(1)}, bf16[2,256,128]{2,1,0:T(8,128)(2,1)S(1)}, u32[]{:S(2)}, u32[]{:S(2)}) %collective-permute-start.35) | collective-permute-done | bytes 131104 | tf_op jit(solution)/shard_map/ppermute | solution.py:17
  184.1 5.5 %collective-permute-done.42 = bf16[2,256,128]{2,1,0:T(8,128)(2,1)S(1)} collective-permute-done((bf16[2,256,128]{2,1,0:T(8,128)(2,1)S(1)}, bf16[2,256,128]{2,1,0:T(8,128)(2,1)S(1)}, u32[]{:S(2)}, u32[]{:S(2)}) %collective-permute-start.42) | collective-permute-done | bytes 131104 | tf_op jit(solution)/shard_map/ppermute | solution.py:17
  (153 shorter events, 66.9 us)
Async XLA Ops:
  3.7 19.0 %collective-permute-start.13 = (bf16[2,64,896]{2,1,0:T(8,128)(2,1)}, bf16[2,64,896]{2,1,0:T(8,128)(2,1)S(1)}, u32[]{:S(2)}, u32[]{:S(2)}) collective-permute-start(bf16[2,64,896]{2,1,0:T(8,128)(2,1)} %get-tuple-element.68), channel_id=1, source_target_pairs={{0,5},{1,4},{2,7},{3,6},{4,1},{5,0},{6,3},{7,2},{8,13},{9,12},{10,... | collective-permute-start | bytes 688136 | tf_op jit(solution)/shard_map/ppermute | solution.py:17
  7.2 21.2 %collective-permute-start.14 = (bf16[2,64,896]{2,1,0:T(8,128)(2,1)}, bf16[2,64,896]{2,1,0:T(8,128)(2,1)S(1)}, u32[]{:S(2)}, u32[]{:S(2)}) collective-permute-start(bf16[2,64,896]{2,1,0:T(8,128)(2,1)} %get-tuple-element.69), channel_id=1, source_target_pairs={{0,4},{1,5},{2,6},{3,7},{4,0},{5,1},{6,2},{7,3},{8,12},{9,13},{10,... | collective-permute-start | bytes 688136 | tf_op jit(solution)/shard_map/ppermute | solution.py:17
  7.8 24.4 %collective-permute-start.15 = (bf16[2,64,896]{2,1,0:T(8,128)(2,1)}, bf16[2,64,896]{2,1,0:T(8,128)(2,1)S(1)}, u32[]{:S(2)}, u32[]{:S(2)}) collective-permute-start(bf16[2,64,896]{2,1,0:T(8,128)(2,1)} %get-tuple-element.70), channel_id=1, source_target_pairs={{0,3},{1,2},{2,1},{3,0},{4,7},{5,6},{6,5},{7,4},{8,11},{9,10},{10,... | collective-permute-start | bytes 688136 | tf_op jit(solution)/shard_map/ppermute | solution.py:17
  9.2 25.7 %collective-permute-start.16 = (bf16[2,64,896]{2,1,0:T(8,128)(2,1)}, bf16[2,64,896]{2,1,0:T(8,128)(2,1)S(1)}, u32[]{:S(2)}, u32[]{:S(2)}) collective-permute-start(bf16[2,64,896]{2,1,0:T(8,128)(2,1)} %get-tuple-element.71), channel_id=1, source_target_pairs={{0,2},{1,3},{2,0},{3,1},{4,6},{5,7},{6,4},{7,5},{8,10},{9,11},{10,... | collective-permute-start | bytes 688136 | tf_op jit(solution)/shard_map/ppermute | solution.py:17
  11.4 41.2 %collective-permute-start = (bf16[4,2,64,1152]{3,2,1,0:T(8,128)(2,1)S(1)}, bf16[4,2,64,1152]{3,2,1,0:T(8,128)(2,1)S(1)}, u32[]{:S(2)}, u32[]{:S(2)}) collective-permute-start(bf16[4,2,64,1152]{3,2,1,0:T(8,128)(2,1)S(1)} %lend_blocks.1), channel_id=1, source_target_pairs={{0,1},{1,0},{2,3},{3,2},{4,5},{5,4},{6,7},{7,6},{8,9},{9,8},{10,11... | collective-permute-start | bytes 3538952 | tf_op jit(solution)/shard_map/ppermute | solution.py:17
  22.7 14.5 %collective-permute-start.17 = (bf16[2,64,896]{2,1,0:T(8,128)(2,1)}, bf16[2,64,896]{2,1,0:T(8,128)(2,1)}, u32[]{:S(2)}, u32[]{:S(2)}) collective-permute-start(bf16[2,64,896]{2,1,0:T(8,128)(2,1)} %copy-done.5), channel_id=1, source_target_pairs={{0,1},{1,0},{2,3},{3,2},{4,5},{5,4},{6,7},{7,6},{8,9},{9,8},{10,11... | collective-permute-start | bytes 688136 | tf_op jit(solution)/shard_map/ppermute | solution.py:17
  32.9 10.8 %collective-permute-start.12 = (bf16[2,64,896]{2,1,0:T(8,128)(2,1)}, bf16[2,64,896]{2,1,0:T(8,128)(2,1)}, u32[]{:S(2)}, u32[]{:S(2)}) collective-permute-start(bf16[2,64,896]{2,1,0:T(8,128)(2,1)} %copy-done.6), channel_id=1, source_target_pairs={{0,6},{1,7},{2,4},{3,5},{4,2},{5,3},{6,0},{7,1},{8,14},{9,15},{10,... | collective-permute-start | bytes 688136 | tf_op jit(solution)/shard_map/ppermute | solution.py:17
  35.5 18.7 %collective-permute-start.7 = (f32[2,4224]{1,0:T(2,128)}, f32[2,4224]{1,0:T(2,128)}, u32[]{:S(2)}, u32[]{:S(2)}) collective-permute-start(f32[2,4224]{1,0:T(2,128)} %get-tuple-element.167), channel_id=1, source_target_pairs={{0,16},{8,24},{16,0},{24,8},{1,17},{9,25},{17,1},{25,9},{2,18},{10... | collective-permute-start | bytes 101384 | tf_op jit(solution)/shard_map/ppermute | solution.py:17
  49.1 37.1 %collective-permute-start.18 = (bf16[2,128,896]{2,1,0:T(8,128)(2,1)}, bf16[2,128,896]{2,1,0:T(8,128)(2,1)S(1)}, u32[]{:S(2)}, u32[]{:S(2)}) collective-permute-start(bf16[2,128,896]{2,1,0:T(8,128)(2,1)} %get-tuple-element.85), channel_id=1, source_target_pairs={{0,8},{8,0},{16,24},{24,16},{1,9},{9,1},{17,25},{25,17},{2,10},{10... | collective-permute-start | bytes 1376264 | tf_op jit(solution)/shard_map/ppermute | solution.py:17
  50.9 35.3 %collective-permute-start.19 = (bf16[2,128,896]{2,1,0:T(8,128)(2,1)}, bf16[2,128,896]{2,1,0:T(8,128)(2,1)}, u32[]{:S(2)}, u32[]{:S(2)}) collective-permute-start(bf16[2,128,896]{2,1,0:T(8,128)(2,1)} %get-tuple-element.86), channel_id=1, source_target_pairs={{0,16},{8,24},{16,0},{24,8},{1,17},{9,25},{17,1},{25,9},{2,18},{10... | collective-permute-start | bytes 1376264 | tf_op jit(solution)/shard_map/ppermute | solution.py:17
  52.5 36.3 %collective-permute-start.20 = (bf16[2,128,896]{2,1,0:T(8,128)(2,1)}, bf16[2,128,896]{2,1,0:T(8,128)(2,1)}, u32[]{:S(2)}, u32[]{:S(2)}) collective-permute-start(bf16[2,128,896]{2,1,0:T(8,128)(2,1)} %get-tuple-element.87), channel_id=1, source_target_pairs={{0,24},{8,16},{16,8},{24,0},{1,25},{9,17},{17,9},{25,1},{2,26},{10... | collective-permute-start | bytes 1376264 | tf_op jit(solution)/shard_map/ppermute | solution.py:17
  56.6 14.1 %collective-permute-start.24 = (bf16[2,2,64,384]{3,2,1,0:T(8,128)(2,1)S(1)}, bf16[2,2,64,384]{3,2,1,0:T(8,128)(2,1)S(1)}, u32[]{:S(2)}, u32[]{:S(2)}) collective-permute-start(bf16[2,2,64,384]{3,2,1,0:T(8,128)(2,1)S(1)} %get-tuple-element.92), channel_id=1, source_target_pairs={{0,6},{1,7},{2,4},{3,5},{4,2},{5,3},{6,0},{7,1},{8,14},{9,15},{10,... | collective-permute-start | bytes 589832 | tf_op jit(solution)/shard_map/ppermute | solution.py:17
  60.5 18.9 %collective-permute-start.25 = (bf16[2,2,64,384]{3,2,1,0:T(8,128)(2,1)S(1)}, bf16[2,2,64,384]{3,2,1,0:T(8,128)(2,1)S(1)}, u32[]{:S(2)}, u32[]{:S(2)}) collective-permute-start(bf16[2,2,64,384]{3,2,1,0:T(8,128)(2,1)S(1)} %get-tuple-element.93), channel_id=1, source_target_pairs={{0,4},{1,5},{2,6},{3,7},{4,0},{5,1},{6,2},{7,3},{8,12},{9,13},{10,... | collective-permute-start | bytes 589832 | tf_op jit(solution)/shard_map/ppermute | solution.py:17
  70.7 13.0 %collective-permute-start.26 = (bf16[2,2,64,384]{3,2,1,0:T(8,128)(2,1)S(1)}, bf16[2,2,64,384]{3,2,1,0:T(8,128)(2,1)S(1)}, u32[]{:S(2)}, u32[]{:S(2)}) collective-permute-start(bf16[2,2,64,384]{3,2,1,0:T(8,128)(2,1)S(1)} %get-tuple-element.94), channel_id=1, source_target_pairs={{0,2},{1,3},{2,0},{3,1},{4,6},{5,7},{6,4},{7,5},{8,10},{9,11},{10,... | collective-permute-start | bytes 589832 | tf_op jit(solution)/shard_map/ppermute | solution.py:17
  79.5 11.2 %collective-permute-start.10 = (bf16[2,2,64,384]{3,2,1,0:T(8,128)(2,1)S(1)}, bf16[2,2,64,384]{3,2,1,0:T(8,128)(2,1)S(1)}, u32[]{:S(2)}, u32[]{:S(2)}) collective-permute-start(bf16[2,2,64,384]{3,2,1,0:T(8,128)(2,1)S(1)} %get-tuple-element.83), channel_id=1, source_target_pairs={{0,2},{1,3},{2,0},{3,1},{4,6},{5,7},{6,4},{7,5},{8,10},{9,11},{10,... | collective-permute-start | bytes 589832 | tf_op jit(solution)/shard_map/ppermute | solution.py:17
  86.1 25.1 %collective-permute-start.9 = (bf16[2,2,64,384]{3,2,1,0:T(8,128)(2,1)S(1)}, bf16[2,2,64,384]{3,2,1,0:T(8,128)(2,1)S(1)}, u32[]{:S(2)}, u32[]{:S(2)}) collective-permute-start(bf16[2,2,64,384]{3,2,1,0:T(8,128)(2,1)S(1)} %get-tuple-element.82), channel_id=1, source_target_pairs={{0,4},{1,5},{2,6},{3,7},{4,0},{5,1},{6,2},{7,3},{8,12},{9,13},{10,... | collective-permute-start | bytes 589832 | tf_op jit(solution)/shard_map/ppermute | solution.py:17
  86.2 27.5 %collective-permute-start.1 = (bf16[2,2,64,384]{3,2,1,0:T(8,128)(2,1)S(1)}, bf16[2,2,64,384]{3,2,1,0:T(8,128)(2,1)S(1)}, u32[]{:S(2)}, u32[]{:S(2)}) collective-permute-start(bf16[2,2,64,384]{3,2,1,0:T(8,128)(2,1)S(1)} %get-tuple-element.59), channel_id=1, source_target_pairs={{0,6},{1,7},{2,4},{3,5},{4,2},{5,3},{6,0},{7,1},{8,14},{9,15},{10,... | collective-permute-start | bytes 589832 | tf_op jit(solution)/shard_map/ppermute | solution.py:17
  88.8 29.6 %collective-permute-start.2 = (bf16[2,2,64,384]{3,2,1,0:T(8,128)(2,1)S(1)}, bf16[2,2,64,384]{3,2,1,0:T(8,128)(2,1)S(1)}, u32[]{:S(2)}, u32[]{:S(2)}) collective-permute-start(bf16[2,2,64,384]{3,2,1,0:T(8,128)(2,1)S(1)} %get-tuple-element.60), channel_id=1, source_target_pairs={{0,4},{1,5},{2,6},{3,7},{4,0},{5,1},{6,2},{7,3},{8,12},{9,13},{10,... | collective-permute-start | bytes 589832 | tf_op jit(solution)/shard_map/ppermute | solution.py:17
  90.6 29.2 %collective-permute-start.3 = (bf16[2,2,64,384]{3,2,1,0:T(8,128)(2,1)S(1)}, bf16[2,2,64,384]{3,2,1,0:T(8,128)(2,1)S(1)}, u32[]{:S(2)}, u32[]{:S(2)}) collective-permute-start(bf16[2,2,64,384]{3,2,1,0:T(8,128)(2,1)S(1)} %get-tuple-element.61), channel_id=1, source_target_pairs={{0,2},{1,3},{2,0},{3,1},{4,6},{5,7},{6,4},{7,5},{8,10},{9,11},{10,... | collective-permute-start | bytes 589832 | tf_op jit(solution)/shard_map/ppermute | solution.py:17
  93.3 28.1 %collective-permute-start.27 = (bf16[2,128,384]{2,1,0:T(8,128)(2,1)S(1)}, bf16[2,128,384]{2,1,0:T(8,128)(2,1)S(1)}, u32[]{:S(2)}, u32[]{:S(2)}) collective-permute-start(bf16[2,128,384]{2,1,0:T(8,128)(2,1)S(1)} %get-tuple-element.96), channel_id=1, source_target_pairs={{0,8},{8,0},{16,24},{24,16},{1,9},{9,1},{17,25},{25,17},{2,10},{10... | collective-permute-start | bytes 589832 | tf_op jit(solution)/shard_map/ppermute | solution.py:17
  111.3 11.6 %collective-permute-start.28 = (bf16[2,128,384]{2,1,0:T(8,128)(2,1)S(1)}, bf16[2,128,384]{2,1,0:T(8,128)(2,1)S(1)}, u32[]{:S(2)}, u32[]{:S(2)}) collective-permute-start(bf16[2,128,384]{2,1,0:T(8,128)(2,1)S(1)} %get-tuple-element.97), channel_id=1, source_target_pairs={{0,16},{8,24},{16,0},{24,8},{1,17},{9,25},{17,1},{25,9},{2,18},{10... | collective-permute-start | bytes 589832 | tf_op jit(solution)/shard_map/ppermute | solution.py:17
  119.9 12.5 %collective-permute-start.22 = (bf16[2,128,384]{2,1,0:T(8,128)(2,1)S(1)}, bf16[2,128,384]{2,1,0:T(8,128)(2,1)S(1)}, u32[]{:S(2)}, u32[]{:S(2)}) collective-permute-start(bf16[2,128,384]{2,1,0:T(8,128)(2,1)S(1)} %get-tuple-element.90), channel_id=1, source_target_pairs={{0,16},{8,24},{16,0},{24,8},{1,17},{9,25},{17,1},{25,9},{2,18},{10... | collective-permute-start | bytes 589832 | tf_op jit(solution)/shard_map/ppermute | solution.py:17
  121.4 11.0 %collective-permute-start.23 = (bf16[2,128,384]{2,1,0:T(8,128)(2,1)S(1)}, bf16[2,128,384]{2,1,0:T(8,128)(2,1)S(1)}, u32[]{:S(2)}, u32[]{:S(2)}) collective-permute-start(bf16[2,128,384]{2,1,0:T(8,128)(2,1)S(1)} %get-tuple-element.91), channel_id=1, source_target_pairs={{0,24},{8,16},{16,8},{24,0},{1,25},{9,17},{17,9},{25,1},{2,26},{10... | collective-permute-start | bytes 589832 | tf_op jit(solution)/shard_map/ppermute | solution.py:17
  122.9 13.1 %collective-permute-start.4 = (bf16[2,128,384]{2,1,0:T(8,128)(2,1)S(1)}, bf16[2,128,384]{2,1,0:T(8,128)(2,1)S(1)}, u32[]{:S(2)}, u32[]{:S(2)}) collective-permute-start(bf16[2,128,384]{2,1,0:T(8,128)(2,1)S(1)} %get-tuple-element.63), channel_id=1, source_target_pairs={{0,8},{8,0},{16,24},{24,16},{1,9},{9,1},{17,25},{25,17},{2,10},{10... | collective-permute-start | bytes 589832 | tf_op jit(solution)/shard_map/ppermute | solution.py:17
  124.4 13.6 %collective-permute-start.5 = (bf16[2,128,384]{2,1,0:T(8,128)(2,1)S(1)}, bf16[2,128,384]{2,1,0:T(8,128)(2,1)S(1)}, u32[]{:S(2)}, u32[]{:S(2)}) collective-permute-start(bf16[2,128,384]{2,1,0:T(8,128)(2,1)S(1)} %get-tuple-element.64), channel_id=1, source_target_pairs={{0,16},{8,24},{16,0},{24,8},{1,17},{9,25},{17,1},{25,9},{2,18},{10... | collective-permute-start | bytes 589832 | tf_op jit(solution)/shard_map/ppermute | solution.py:17
  125.9 12.1 %collective-permute-start.6 = (bf16[2,128,384]{2,1,0:T(8,128)(2,1)S(1)}, bf16[2,128,384]{2,1,0:T(8,128)(2,1)S(1)}, u32[]{:S(2)}, u32[]{:S(2)}) collective-permute-start(bf16[2,128,384]{2,1,0:T(8,128)(2,1)S(1)} %get-tuple-element.65), channel_id=1, source_target_pairs={{0,24},{8,16},{16,8},{24,0},{1,25},{9,17},{17,9},{25,1},{2,26},{10... | collective-permute-start | bytes 589832 | tf_op jit(solution)/shard_map/ppermute | solution.py:17
  150.4 11.7 %collective-permute-start.33 = (bf16[4,2,256,128]{3,2,1,0:T(8,128)(2,1)S(1)}, bf16[4,2,256,128]{3,2,1,0:T(8,128)(2,1)S(1)}, u32[]{:S(2)}, u32[]{:S(2)}) collective-permute-start(bf16[4,2,256,128]{3,2,1,0:T(8,128)(2,1)S(1)} %get-tuple-element.104), channel_id=1, source_target_pairs={{0,1},{1,0},{2,3},{3,2},{4,5},{5,4},{6,7},{7,6},{8,9},{9,8},{10,11... | collective-permute-start | bytes 1572872 | tf_op jit(solution)/shard_map/ppermute | solution.py:17
  163.8 20.2 %collective-permute-start.35 = (bf16[2,256,128]{2,1,0:T(8,128)(2,1)S(1)}, bf16[2,256,128]{2,1,0:T(8,128)(2,1)S(1)}, u32[]{:S(2)}, u32[]{:S(2)}) collective-permute-start(bf16[2,256,128]{2,1,0:T(8,128)(2,1)S(1)} %get-tuple-element.119), channel_id=1, source_target_pairs={{0,4},{1,5},{2,6},{3,7},{4,0},{5,1},{6,2},{7,3},{8,12},{9,13},{10,... | collective-permute-start | bytes 393224 | tf_op jit(solution)/shard_map/ppermute | solution.py:17
  166.1 17.9 %collective-permute-start.36 = (bf16[2,256,128]{2,1,0:T(8,128)(2,1)S(1)}, bf16[2,256,128]{2,1,0:T(8,128)(2,1)S(1)}, u32[]{:S(2)}, u32[]{:S(2)}) collective-permute-start(bf16[2,256,128]{2,1,0:T(8,128)(2,1)S(1)} %get-tuple-element.118), channel_id=1, source_target_pairs={{0,2},{1,3},{2,0},{3,1},{4,6},{5,7},{6,4},{7,5},{8,10},{9,11},{10,... | collective-permute-start | bytes 393224 | tf_op jit(solution)/shard_map/ppermute | solution.py:17
  166.8 17.4 %collective-permute-start.41 = (bf16[2,256,128]{2,1,0:T(8,128)(2,1)S(1)}, bf16[2,256,128]{2,1,0:T(8,128)(2,1)S(1)}, u32[]{:S(2)}, u32[]{:S(2)}) collective-permute-start(bf16[2,256,128]{2,1,0:T(8,128)(2,1)S(1)} %get-tuple-element.120), channel_id=1, source_target_pairs={{0,6},{1,7},{2,4},{3,5},{4,2},{5,3},{6,0},{7,1},{8,14},{9,15},{10,... | collective-permute-start | bytes 393224 | tf_op jit(solution)/shard_map/ppermute | solution.py:17
  168.7 20.9 %collective-permute-start.42 = (bf16[2,256,128]{2,1,0:T(8,128)(2,1)S(1)}, bf16[2,256,128]{2,1,0:T(8,128)(2,1)S(1)}, u32[]{:S(2)}, u32[]{:S(2)}) collective-permute-start(bf16[2,256,128]{2,1,0:T(8,128)(2,1)S(1)} %get-tuple-element.122), channel_id=1, source_target_pairs={{0,4},{1,5},{2,6},{3,7},{4,0},{5,1},{6,2},{7,3},{8,12},{9,13},{10,... | collective-permute-start | bytes 393224 | tf_op jit(solution)/shard_map/ppermute | solution.py:17
  170.5 19.1 %collective-permute-start.43 = (bf16[2,256,128]{2,1,0:T(8,128)(2,1)S(1)}, bf16[2,256,128]{2,1,0:T(8,128)(2,1)S(1)}, u32[]{:S(2)}, u32[]{:S(2)}) collective-permute-start(bf16[2,256,128]{2,1,0:T(8,128)(2,1)S(1)} %get-tuple-element.121), channel_id=1, source_target_pairs={{0,2},{1,3},{2,0},{3,1},{4,6},{5,7},{6,4},{7,5},{8,10},{9,11},{10,... | collective-permute-start | bytes 393224 | tf_op jit(solution)/shard_map/ppermute | solution.py:17
  (24 other events, 117.0 us)
